TPU v7x, 512 devices: a whole 4x4x16 slice. The times are simulated.
512 devices in a mesh: rows: 32 (over x, y, core), cols: 16 (over z).
Axes of the slice: x: 4, y: 4, z: 16, core: 2. Of those that a mesh axis runs over, the one named last changes fastest.
Arguments:
- coadd_flux: float32 [4096, 16384], P('rows', 'cols'), may hold values from -8 to 8
- inverse_variance: float32 [4096, 16384], P('rows', 'cols'), may hold values from 0.25 to 4
- source_mask: int32 [4096, 16384], P('rows', 'cols'), may hold values 0 or 1
Outputs:
- background: float32 [4096, 16384], P('rows', 'cols')
- rms_map: float32 [4096, 16384], P('rows', 'cols')
All inputs are finite; a program needn't handle non-finite values. No bound on the sum of `source_mask` on one device may be relied on, other than what follows from the above.
Results may differ from a plain program's by a relative error of at most 0.0001.
Values sent between devices are 32-bit elements; how exact they have to be, the bound alone decides.
A program may use at most 64 MiB of HBM per device.

v0:
```python
import jax
import jax.numpy as jnp
from jax import lax
from jax.sharding import PartitionSpec as P

ITERS = 2
RADIUS = 32


smooth_weight = 2.0
blur_sigma = 10.0


def padded_2(block, sides, width):
    for axis, dim in sides:
        count = lax.axis_size(axis)
        forward = [(i, i + 1) for i in range(count - 1)]
        backward = [(target, source) for source, target in forward]
        low = lax.ppermute(
            lax.slice_in_dim(block, block.shape[dim] - width, None, axis=dim), axis, forward
        )
        high = lax.ppermute(lax.slice_in_dim(block, 0, width, axis=dim), axis, backward)
        block = jnp.concatenate([low, block, high], axis=dim)
    return block


def stencil_local(padded, field, weight):
    beside = padded[2:, 1:-1] + padded[:-2, 1:-1] + padded[1:-1, 2:] + padded[1:-1, :-2]
    return weight * field + smooth_weight * (4.0 * field - beside)


def apply_operator(field, weight):
    padded = padded_2(field, (("rows", 0), ("cols", 1)), 1)
    return stencil_local(padded, field, weight)


def tap_table(out_length):
    offsets = jnp.arange(2 * RADIUS + 1).astype(jnp.float32) - RADIUS
    raw_taps = jnp.exp(-offsets * offsets / (2.0 * blur_sigma * blur_sigma))
    norm_taps = jnp.sum(raw_taps)
    shape = (out_length, out_length + 2 * RADIUS)
    row_index = lax.broadcasted_iota(jnp.int32, shape, 0)
    col_index = lax.broadcasted_iota(jnp.int32, shape, 1)
    spread = col_index - row_index
    inside = (spread >= 0) & (spread <= 2 * RADIUS)
    centred = (spread - RADIUS).astype(jnp.float32)
    values = jnp.exp(-centred * centred / (2.0 * blur_sigma * blur_sigma)) / norm_taps
    return jnp.where(inside, values, 0.0)


def rows_apply(extended, out_length):
    return jnp.dot(tap_table(out_length), extended, precision=lax.Precision.HIGHEST)


def cols_apply(extended, out_length):
    return jnp.dot(extended, tap_table(out_length).T, precision=lax.Precision.HIGHEST)


def pass_rows(field):
    extended = padded_2(field, (("rows", 0),), RADIUS)
    return rows_apply(extended, field.shape[0])


def pass_cols(field):
    extended = padded_2(field, (("cols", 1),), RADIUS)
    return cols_apply(extended, field.shape[1])


def shards(coadd_flux, inverse_variance, source_mask):
    weight = inverse_variance * (1.0 - source_mask.astype(jnp.float32))

    def squares(residual):
        return lax.psum(jnp.sum(residual * residual), ("rows", "cols"))

    background = jnp.zeros_like(coadd_flux)
    residual = weight * coadd_flux
    direction = residual
    norm_now = squares(residual)
    for step in range(ITERS):
        image_term = apply_operator(direction, weight)
        alpha = norm_now / lax.psum(jnp.sum(direction * image_term), ("rows", "cols"))
        background = background + alpha * direction
        residual = residual - alpha * image_term
        if step + 1 < ITERS:
            norm_next = squares(residual)
            direction = residual + norm_next / norm_now * direction
            norm_now = norm_next
    scatter = coadd_flux - background
    smoothed = scatter * scatter
    for repeat in range(2):
        smoothed = pass_rows(smoothed)
        smoothed = pass_cols(smoothed)
    return (background, jnp.sqrt(smoothed + 1e-06))


def solution(mesh):
    return jax.shard_map(
        shards,
        mesh=mesh,
        in_specs=(P("rows", "cols"), P("rows", "cols"), P("rows", "cols")),
        out_specs=(P("rows", "cols"), P("rows", "cols")),
        check_vma=False,
    )
```

profile of v0, /device:TPU:1, one launch (start us, length us, event | category | flops | bytes accessed | tf_op | source)
XLA Modules:
  0.0 402.4 jit_solution(13780213059941160279)
XLA Ops:
  0.6 0.0 copy-start.1
  0.6 1.5 fusion.77
  2.2 0.0 copy-start
  2.2 4.7 %collective-permute-start.1 = (f32[1,1024]{1,0:T(1,128)S(1)}, f32[1,1024]{1,0:T(1,128)S(1)}, u32[]{:S(2)}, u32[]{:S(2)}) collective-permute-start(f32[1,1024]{1,0:T(1,128)S(1)} %get-tuple-element.23), channel_id=1, source_target_pairs={{0,16},{16,32},{32,48},{48,64},{64,80},{80,96},{96,112},{112,128},... | collective-permute-start | bytes 12296 | tf_op jit(solution)/shard_map/ppermute | solution.py:19
  6.9 5.5 %collective-permute-start = (f32[1,1024]{1,0:T(1,128)S(1)}, f32[1,1024]{1,0:T(1,128)S(1)}, u32[]{:S(2)}, u32[]{:S(2)}) collective-permute-start(f32[1,1024]{1,0:T(1,128)S(1)} %get-tuple-element.24), channel_id=1, source_target_pairs={{16,0},{32,16},{48,32},{64,48},{80,64},{96,80},{112,96},{128,112},... | collective-permute-start | bytes 12296 | tf_op jit(solution)/shard_map/ppermute | solution.py:22
  12.4 0.0 collective-permute-done.1
  12.4 0.8 collective-permute-done
  13.2 0.1 pad_maximum_fusion.21
  13.3 1.3 collective-permute-start.2
  14.6 4.0 collective-permute-start.3
  18.6 0.0 collective-permute-done.2
  18.6 1.3 collective-permute-done.3
  20.0 0.0 copy-done.1
  20.0 0.0 copy-done
  20.0 1.1 multiply_reduce_fusion.1
  21.1 110.6 %all-reduce = (f32[]{:T(128)}, f32[]{:T(128)}) all-reduce(f32[]{:T(128)} %get-tuple-element.3, f32[]{:T(128)} %get-tuple-element.2), channel_id=1, replica_groups=mesh['rows'=32,'cols'=16] {'rows','cols'}, use_global_device_ids=true, to_apply=%region_1.0 | all-reduce | flops 2 | bytes 16 | tf_op jit(solution)/shard_map/psum | solution.py:73
  133.0 0.7 multiply_reduce_fusion
  133.7 100.8 %psum.30 = f32[]{:T(128)} all-reduce(f32[]{:T(128)} %multiply_reduce_fusion), channel_id=1, replica_groups=mesh['rows'=32,'cols'=16] {'rows','cols'}, use_global_device_ids=true, to_apply=%region_5.0 | all-reduce | flops 1 | bytes 8 | tf_op jit(solution)/shard_map/psum | solution.py:73
  235.8 0.1 multiply_add_fusion.1
  235.9 3.4 collective-permute-start.5
  239.3 1.9 collective-permute-start.4
  241.3 0.0 collective-permute-done.5
  241.3 3.0 collective-permute-done.4
  244.3 0.1 pad_maximum_fusion.18
  244.4 1.3 collective-permute-start.6
  245.7 0.0 copy-start.2
  245.7 4.1 %collective-permute-start.7 = (f32[130,1]{1,0:T(8,128)S(1)}, f32[130,1]{1,0:T(8,128)S(1)}, u32[]{:S(2)}, u32[]{:S(2)}) collective-permute-start(f32[130,1]{1,0:T(8,128)S(1)} %get-tuple-element.10), channel_id=1, source_target_pairs={{0,1},{1,2},{2,3},{3,4},{4,5},{5,6},{6,7},{7,8},{8,9},{9,10},{10,1... | collective-permute-start | bytes 1568 | tf_op jit(solution)/shard_map/ppermute | solution.py:19
  249.8 0.0 collective-permute-done.6
  249.8 1.3 collective-permute-done.7
  251.1 1.1 fusion.34
  252.3 102.9 %psum.31 = f32[]{:T(128)} all-reduce(f32[]{:T(128)} %fusion.34), channel_id=1, replica_groups=mesh['rows'=32,'cols'=16] {'rows','cols'}, use_global_device_ids=true, to_apply=%region_7.0 | all-reduce | flops 1 | bytes 8 | tf_op jit(solution)/shard_map/psum | solution.py:81
  356.5 0.0 copy-done.2
  356.5 1.0 subtract_multiply_fusion
  357.5 3.7 collective-permute-start.8
  361.2 1.9 collective-permute-start.9
  363.2 0.7 fusion.54
  363.9 0.0 collective-permute-done.8
  363.9 3.7 collective-permute-done.9
  367.5 1.4 fusion.17
  368.9 0.1 fusion.81
  369.0 1.3 collective-permute-start.11
  370.3 4.0 collective-permute-start.10
  374.3 0.0 collective-permute-done.11
  374.3 1.3 collective-permute-done.10
  375.6 0.3 concatenate.55
  375.9 3.7 fusion.9
  379.6 2.9 collective-permute-start.12
  382.5 1.9 collective-permute-start.13
  384.5 0.0 collective-permute-done.12
  384.5 4.3 %collective-permute-done.13 = f32[32,1024]{1,0:T(8,128)S(1)} collective-permute-done((f32[32,1024]{1,0:T(8,128)S(1)}, f32[32,1024]{1,0:T(8,128)S(1)}, u32[]{:S(2)}, u32[]{:S(2)}) %collective-permute-start.13) | collective-permute-done | bytes 131104 | tf_op jit(solution)/shard_map/ppermute | solution.py:22
  388.8 1.4 fusion.23
  390.2 0.1 fusion.79
  390.3 1.3 collective-permute-start.15
  391.6 4.8 %collective-permute-start.14 = (f32[128,32]{1,0:T(8,128)S(1)}, f32[128,32]{1,0:T(8,128)S(1)}, u32[]{:S(2)}, u32[]{:S(2)}) collective-permute-start(f32[128,32]{1,0:T(8,128)S(1)} %get-tuple-element.14), channel_id=1, source_target_pairs={{0,1},{1,2},{2,3},{3,4},{4,5},{5,6},{6,7},{7,8},{8,9},{9,10},{10,1... | collective-permute-start | bytes 49160 | tf_op jit(solution)/shard_map/ppermute | solution.py:19
  396.4 0.0 collective-permute-done.15
  396.4 1.1 collective-permute-done.14
  397.5 0.3 concatenate.57
  397.8 4.5 %fusion.14 = f32[128,1024]{1,0:T(8,128)} fusion(f32[128,1088]{1,0:T(8,128)S(1)} %concatenate.57, f32[]{:T(128)} %fusion.54), kind=kOutput, calls=%fused_computation.12 | convolution fusion | flops 1723662336 | bytes 1081348 | tf_op jit(solution)/shard_map/dot_general | solution.py:56
  (4 shorter events, 0.1 us)
Async XLA Ops:
  0.6 19.3 %copy-start.1 = (s32[128,1024]{1,0:T(8,128)S(1)}, s32[128,1024]{1,0:T(8,128)}, u32[]{:S(2)}) copy-start(s32[128,1024]{1,0:T(8,128)} %param.5) | copy-start | bytes 1572868
  2.2 17.8 %copy-start = (f32[128,1024]{1,0:T(8,128)S(1)}, f32[128,1024]{1,0:T(8,128)}, u32[]{:S(2)}) copy-start(f32[128,1024]{1,0:T(8,128)} %param.4) | copy-start | bytes 1572868
  2.2 10.2 %collective-permute-start.1 = (f32[1,1024]{1,0:T(1,128)S(1)}, f32[1,1024]{1,0:T(1,128)S(1)}, u32[]{:S(2)}, u32[]{:S(2)}) collective-permute-start(f32[1,1024]{1,0:T(1,128)S(1)} %get-tuple-element.23), channel_id=1, source_target_pairs={{0,16},{16,32},{32,48},{48,64},{64,80},{80,96},{96,112},{112,128},... | collective-permute-start | bytes 12296 | tf_op jit(solution)/shard_map/ppermute | solution.py:19
  6.9 6.3 %collective-permute-start = (f32[1,1024]{1,0:T(1,128)S(1)}, f32[1,1024]{1,0:T(1,128)S(1)}, u32[]{:S(2)}, u32[]{:S(2)}) collective-permute-start(f32[1,1024]{1,0:T(1,128)S(1)} %get-tuple-element.24), channel_id=1, source_target_pairs={{16,0},{32,16},{48,32},{64,48},{80,64},{96,80},{112,96},{128,112},... | collective-permute-start | bytes 12296 | tf_op jit(solution)/shard_map/ppermute | solution.py:22
  13.3 5.3 %collective-permute-start.2 = (f32[130,1]{1,0:T(8,128)S(1)}, f32[130,1]{1,0:T(8,128)S(1)}, u32[]{:S(2)}, u32[]{:S(2)}) collective-permute-start(f32[130,1]{1,0:T(8,128)S(1)} %get-tuple-element.11), channel_id=1, source_target_pairs={{1,0},{2,1},{3,2},{4,3},{5,4},{6,5},{7,6},{8,7},{9,8},{10,9},{11,1... | collective-permute-start | bytes 1568 | tf_op jit(solution)/shard_map/ppermute | solution.py:22
  14.6 5.3 %collective-permute-start.3 = (f32[130,1]{1,0:T(8,128)S(1)}, f32[130,1]{1,0:T(8,128)S(1)}, u32[]{:S(2)}, u32[]{:S(2)}) collective-permute-start(f32[130,1]{1,0:T(8,128)S(1)} %get-tuple-element.12), channel_id=1, source_target_pairs={{0,1},{1,2},{2,3},{3,4},{4,5},{5,6},{6,7},{7,8},{8,9},{9,10},{10,1... | collective-permute-start | bytes 1568 | tf_op jit(solution)/shard_map/ppermute | solution.py:19
  235.9 5.3 %collective-permute-start.5 = (f32[1,1024]{1,0:T(1,128)S(1)}, f32[1,1024]{1,0:T(1,128)S(1)}, u32[]{:S(2)}, u32[]{:S(2)}) collective-permute-start(f32[1,1024]{1,0:T(1,128)S(1)} %get-tuple-element.21), channel_id=1, source_target_pairs={{0,16},{16,32},{32,48},{48,64},{64,80},{80,96},{96,112},{112,128},... | collective-permute-start | bytes 12296 | tf_op jit(solution)/shard_map/ppermute | solution.py:19
  239.3 4.9 %collective-permute-start.4 = (f32[1,1024]{1,0:T(1,128)S(1)}, f32[1,1024]{1,0:T(1,128)S(1)}, u32[]{:S(2)}, u32[]{:S(2)}) collective-permute-start(f32[1,1024]{1,0:T(1,128)S(1)} %get-tuple-element.22), channel_id=1, source_target_pairs={{16,0},{32,16},{48,32},{64,48},{80,64},{96,80},{112,96},{128,112},... | collective-permute-start | bytes 12296 | tf_op jit(solution)/shard_map/ppermute | solution.py:22
  244.4 5.4 %collective-permute-start.6 = (f32[130,1]{1,0:T(8,128)S(1)}, f32[130,1]{1,0:T(8,128)S(1)}, u32[]{:S(2)}, u32[]{:S(2)}) collective-permute-start(f32[130,1]{1,0:T(8,128)S(1)} %get-tuple-element.9), channel_id=1, source_target_pairs={{1,0},{2,1},{3,2},{4,3},{5,4},{6,5},{7,6},{8,7},{9,8},{10,9},{11,1... | collective-permute-start | bytes 1568 | tf_op jit(solution)/shard_map/ppermute | solution.py:22
  245.7 110.9 %copy-start.2 = (f32[128,1024]{1,0:T(8,128)S(1)}, f32[128,1024]{1,0:T(8,128)}, u32[]{:S(2)}) copy-start(f32[128,1024]{1,0:T(8,128)} %param.3) | copy-start | bytes 1572868
  245.7 5.5 %collective-permute-start.7 = (f32[130,1]{1,0:T(8,128)S(1)}, f32[130,1]{1,0:T(8,128)S(1)}, u32[]{:S(2)}, u32[]{:S(2)}) collective-permute-start(f32[130,1]{1,0:T(8,128)S(1)} %get-tuple-element.10), channel_id=1, source_target_pairs={{0,1},{1,2},{2,3},{3,4},{4,5},{5,6},{6,7},{7,8},{8,9},{9,10},{10,1... | collective-permute-start | bytes 1568 | tf_op jit(solution)/shard_map/ppermute | solution.py:19
  357.5 6.3 %collective-permute-start.8 = (f32[32,1024]{1,0:T(8,128)S(1)}, f32[32,1024]{1,0:T(8,128)S(1)}, u32[]{:S(2)}, u32[]{:S(2)}) collective-permute-start(f32[32,1024]{1,0:T(8,128)S(1)} %get-tuple-element.19), channel_id=1, source_target_pairs={{0,16},{16,32},{32,48},{48,64},{64,80},{80,96},{96,112},{112,128},... | collective-permute-start | bytes 393224 | tf_op jit(solution)/shard_map/ppermute | solution.py:19
  361.2 6.3 %collective-permute-start.9 = (f32[32,1024]{1,0:T(8,128)S(1)}, f32[32,1024]{1,0:T(8,128)S(1)}, u32[]{:S(2)}, u32[]{:S(2)}) collective-permute-start(f32[32,1024]{1,0:T(8,128)S(1)} %get-tuple-element.20), channel_id=1, source_target_pairs={{16,0},{32,16},{48,32},{64,48},{80,64},{96,80},{112,96},{128,112},... | collective-permute-start | bytes 393224 | tf_op jit(solution)/shard_map/ppermute | solution.py:22
  369.0 5.3 %collective-permute-start.11 = (f32[128,32]{1,0:T(8,128)S(1)}, f32[128,32]{1,0:T(8,128)S(1)}, u32[]{:S(2)}, u32[]{:S(2)}) collective-permute-start(f32[128,32]{1,0:T(8,128)S(1)} %get-tuple-element.17), channel_id=1, source_target_pairs={{1,0},{2,1},{3,2},{4,3},{5,4},{6,5},{7,6},{8,7},{9,8},{10,9},{11,1... | collective-permute-start | bytes 49160 | tf_op jit(solution)/shard_map/ppermute | solution.py:22
  370.3 5.3 %collective-permute-start.10 = (f32[128,32]{1,0:T(8,128)S(1)}, f32[128,32]{1,0:T(8,128)S(1)}, u32[]{:S(2)}, u32[]{:S(2)}) collective-permute-start(f32[128,32]{1,0:T(8,128)S(1)} %get-tuple-element.18), channel_id=1, source_target_pairs={{0,1},{1,2},{2,3},{3,4},{4,5},{5,6},{6,7},{7,8},{8,9},{9,10},{10,1... | collective-permute-start | bytes 49160 | tf_op jit(solution)/shard_map/ppermute | solution.py:19
  379.6 4.8 %collective-permute-start.12 = (f32[32,1024]{1,0:T(8,128)S(1)}, f32[32,1024]{1,0:T(8,128)S(1)}, u32[]{:S(2)}, u32[]{:S(2)}) collective-permute-start(f32[32,1024]{1,0:T(8,128)S(1)} %get-tuple-element.15), channel_id=1, source_target_pairs={{0,16},{16,32},{32,48},{48,64},{64,80},{80,96},{96,112},{112,128},... | collective-permute-start | bytes 393224 | tf_op jit(solution)/shard_map/ppermute | solution.py:19
  382.5 6.3 %collective-permute-start.13 = (f32[32,1024]{1,0:T(8,128)S(1)}, f32[32,1024]{1,0:T(8,128)S(1)}, u32[]{:S(2)}, u32[]{:S(2)}) collective-permute-start(f32[32,1024]{1,0:T(8,128)S(1)} %get-tuple-element.16), channel_id=1, source_target_pairs={{16,0},{32,16},{48,32},{64,48},{80,64},{96,80},{112,96},{128,112},... | collective-permute-start | bytes 393224 | tf_op jit(solution)/shard_map/ppermute | solution.py:22
  390.3 6.1 %collective-permute-start.15 = (f32[128,32]{1,0:T(8,128)S(1)}, f32[128,32]{1,0:T(8,128)S(1)}, u32[]{:S(2)}, u32[]{:S(2)}) collective-permute-start(f32[128,32]{1,0:T(8,128)S(1)} %get-tuple-element.13), channel_id=1, source_target_pairs={{1,0},{2,1},{3,2},{4,3},{5,4},{6,5},{7,6},{8,7},{9,8},{10,9},{11,1... | collective-permute-start | bytes 49160 | tf_op jit(solution)/shard_map/ppermute | solution.py:22
  391.6 5.9 %collective-permute-start.14 = (f32[128,32]{1,0:T(8,128)S(1)}, f32[128,32]{1,0:T(8,128)S(1)}, u32[]{:S(2)}, u32[]{:S(2)}) collective-permute-start(f32[128,32]{1,0:T(8,128)S(1)} %get-tuple-element.14), channel_id=1, source_target_pairs={{0,1},{1,2},{2,3},{3,4},{4,5},{5,6},{6,7},{7,8},{8,9},{9,10},{10,1... | collective-permute-start | bytes 49160 | tf_op jit(solution)/shard_map/ppermute | solution.py:19
where the time goes:
time: 407 us; the launch traced here: 402 us
  blocking collectives  314 us (77%)
  starting transfers between devices  48 us (12%)
  waiting for transfers between devices  16.9 us (4%)
  matrix products  10.9 us (3%)
  other arithmetic  6.39 us (2%)
  between operations  4.97 us (1%)
    psum x2, blocking collectives, squares(): return lax.psum(jnp.sum(residual * residual), ('rows', 'cols'))  211 us
    psum x1, blocking collectives, shards(): lax.psum(jnp.sum(direction * image_term), ('rows', 'cols'))  103 us
    ppermute x8, starting transfers between devices, padded_2(): lax.ppermute(lax.slice_in_dim(block, block.shape[dim] - width, None, axis...  31.6 us
    ppermute x8, starting transfers between devices, padded_2(): lax.ppermute(lax.slice_in_dim(block, 0, width, axis=dim), axis, backward)  16.4 us
    ppermute x8, waiting for transfers between devices, padded_2(): lax.ppermute(lax.slice_in_dim(block, 0, width, axis=dim), axis, backward)  11.8 us
    dot_general x2, matrix products, cols_apply(): jnp.dot(extended, tap_table(out_length).T, precision=lax.Precision.HIGHEST)  8.23 us
  transfers between devices with their start and end apart: 16, of which 8 were waited for; matrix products, arithmetic and copies ran while one was open for 0% of the time, Pallas kernels for 0%

commit v1 on v0

v1 whole, which is shorter than its diff:
```python
import functools

import jax
import jax.numpy as jnp
import numpy as np
from jax import lax
from jax.experimental import pallas as pl
from jax.experimental.pallas import tpu as pltpu
from jax.sharding import PartitionSpec as P

RADIUS = 32
SIGMA = 10.0
SMOOTH = 2.0
REACH = 2 * RADIUS
ROWS, COLS = 32, 16
H, W = 128, 1024
HB = 72
LANE = 128
EW = W + 2 * LANE
BH = H + 2 * HB
SH, SW = H + 2 * REACH, W + 2 * REACH
PH = H + 24
MESH = pl.DeviceIdType.MESH
TAP_SUM = float(np.sum(np.exp(-np.arange(-RADIUS, RADIUS + 1) ** 2 / (2.0 * SIGMA * SIGMA))))
F32 = jnp.float32
BF16 = jnp.bfloat16


def tap(distance):
    d = distance.astype(F32)
    value = jnp.exp(-d * d / (2.0 * SIGMA * SIGMA)) / TAP_SUM
    return jnp.where(jnp.abs(distance) <= RADIUS, value, 0.0)


def iota(shape, dim):
    return lax.broadcasted_iota(jnp.int32, shape, dim)


def split(x):
    high = x.astype(BF16)
    return high, (x - high.astype(F32)).astype(BF16)


def dot32(a, b):
    return jnp.dot(a, b, precision=lax.Precision.HIGHEST, preferred_element_type=F32)


def total(x):
    return jnp.sum(jnp.sum(x, axis=0, keepdims=True), axis=1, keepdims=True)


def gather_kernel(
    f_hbm, iv_hbm, mk_hbm,
    fx, ux, vx, uc, vc, row_taps, col_taps, sums,
    fb, wb, ub, ivb, mkb, up, wp, vp, col_out, col_in, msg, slots_p, slots_z,
    load_sem, near_send, near_recv, wide_send, wide_recv, p_send, p_recv, z_send, z_recv,
):
    r, z = lax.axis_index("rows"), lax.axis_index("cols")
    r_up, r_dn = lax.rem(r + ROWS - 1, ROWS), lax.rem(r + 1, ROWS)
    z_lf, z_rt = lax.rem(z + COLS - 1, COLS), lax.rem(z + 1, COLS)
    has_up, has_dn, has_lf, has_rt = r > 0, r < ROWS - 1, z > 0, z < COLS - 1

    loads = [
        pltpu.make_async_copy(f_hbm, fb.at[pl.ds(HB, H), pl.ds(LANE, W)], load_sem.at[0]),
        pltpu.make_async_copy(iv_hbm, ivb, load_sem.at[1]),
        pltpu.make_async_copy(mk_hbm, mkb, load_sem.at[2]),
    ]
    for c in loads:
        c.start()
    up[0:8, :] = jnp.zeros((8, EW), F32)
    up[H + 8 : PH, :] = jnp.zeros((16, EW), F32)
    wp[H + 8 : PH, :] = jnp.zeros((16, EW), F32)

    barrier = pltpu.get_barrier_semaphore()
    count = 0
    for k in range(1, ROWS):
        pl.semaphore_signal(barrier, inc=1, device_id=(lax.rem(r + k, ROWS), z), device_id_type=MESH)
        count += 1
    for k in range(1, COLS):
        pl.semaphore_signal(barrier, inc=1, device_id=(r, lax.rem(z + k, COLS)), device_id_type=MESH)
        count += 1
    for a in (r_up, r_dn):
        for b in (z_lf, z_rt):
            pl.semaphore_signal(barrier, inc=1, device_id=(a, b), device_id_type=MESH)
            count += 1

    for c in loads:
        c.wait()

    def weigh(s, _):
        rows = pl.ds(pl.multiple_of(s * 8, 8), 8)
        w = ivb[rows, :] * (1.0 - mkb[rows, :].astype(F32))
        wb[pl.ds(pl.multiple_of(s * 8 + HB, 8), 8), LANE : LANE + W] = w
        here = pl.ds(pl.multiple_of(s * 8 + 8, 8), 8)
        wp[here, LANE : LANE + W] = w
        u = w * fb[pl.ds(pl.multiple_of(s * 8 + HB, 8), 8), LANE : LANE + W]
        up[here, LANE : LANE + W] = u
        uc[rows, :] = u
        return 0

    lax.fori_loop(0, H // 8, weigh, 0)
    left_cols = jnp.transpose(up[8 : H + 8, LANE : 2 * LANE])
    col_out[0] = left_cols[0:8, :]
    col_out[1] = jnp.transpose(wp[8 : H + 8, LANE : 2 * LANE])[0:8, :]
    col_out[2] = jnp.transpose(up[8 : H + 8, W : W + LANE])[LANE - 8 : LANE, :]

    pl.semaphore_wait(barrier, count)

    near = []

    def near_copy(src, dst, device, send_if, recv_if):
        k = len(near)
        c = pltpu.make_async_remote_copy(
            src_ref=src, dst_ref=dst, send_sem=near_send.at[k], recv_sem=near_recv.at[k],
            device_id=device, device_id_type=MESH,
        )
        near.append((c, send_if, recv_if))

    first, last = pl.ds(8, 8), pl.ds(H, 8)
    top, below = pl.ds(0, 8), pl.ds(H + 8, 8)
    mid, lf, rt = pl.ds(LANE, W), pl.ds(0, LANE), pl.ds(LANE + W, LANE)
    c_first, c_last = pl.ds(LANE, LANE), pl.ds(W, LANE)
    near_copy(up.at[first, mid], up.at[below, mid], (r_up, z), has_up, has_dn)
    near_copy(wp.at[first, mid], wp.at[below, mid], (r_up, z), has_up, has_dn)
    near_copy(up.at[last, mid], up.at[top, mid], (r_dn, z), has_dn, has_up)
    near_copy(col_out.at[0], col_in.at[0], (r, z_lf), has_lf, has_rt)
    near_copy(col_out.at[1], col_in.at[1], (r, z_lf), has_lf, has_rt)
    near_copy(col_out.at[2], col_in.at[2], (r, z_rt), has_rt, has_lf)
    near_copy(up.at[last, c_first], up.at[top, rt], (r_dn, z_lf), has_dn & has_lf, has_up & has_rt)
    near_copy(up.at[first, c_first], up.at[below, rt], (r_up, z_lf), has_up & has_lf, has_dn & has_rt)
    near_copy(up.at[first, c_last], up.at[below, lf], (r_up, z_rt), has_up & has_rt, has_dn & has_lf)
    for c, send_if, _ in near:
        pl.when(send_if)(c.start)
    for c, _, recv_if in near:
        pl.when(recv_if)(c.wait_recv)

    pad = jnp.zeros((LANE - 8, LANE), F32)

    def column(x, there):
        return jnp.where(there, x, jnp.zeros_like(x))

    up[8 : H + 8, LANE + W : EW] = jnp.transpose(jnp.concatenate([column(col_in[0], has_rt), pad], axis=0))
    wp[8 : H + 8, LANE + W : EW] = jnp.transpose(jnp.concatenate([column(col_in[1], has_rt), pad], axis=0))
    up[8 : H + 8, 0:LANE] = jnp.transpose(jnp.concatenate([pad, column(col_in[2], has_lf)], axis=0))

    cols8 = iota((8, EW), 1) - LANE
    rows8 = iota((8, EW), 0)

    def higher(src, row, x):
        before = src[pl.ds(pl.multiple_of(row - 8, 8), 8), :]
        return pltpu.roll(jnp.where(rows8 == 7, before, x), 1, 0)

    def lower(src, row, x):
        after = src[pl.ds(pl.multiple_of(row + 8, 8), 8), :]
        return pltpu.roll(jnp.where(rows8 == 0, after, x), 7, 0)

    def operator(src, row, u, w):
        above, under = higher(src, row, u), lower(src, row, u)
        beside = above + under + pltpu.roll(u, 1, 1) + pltpu.roll(u, EW - 1, 1)
        return w * u + SMOOTH * (4.0 * u - beside)

    def image(s, _):
        row = pl.multiple_of(s * 8 + 8, 8)
        here = pl.ds(row, 8)
        v = operator(up, row, up[here, :], wp[here, :])
        inside = ((rows8 + s * 8 < H) | has_dn) & ((cols8 < W) | has_rt)
        vp[here, :] = jnp.where(inside, v, 0.0)
        return 0

    lax.fori_loop(0, H // 8 + 1, image, 0)

    def add_up(s, acc):
        row = pl.multiple_of(s * 8 + 8, 8)
        here = pl.ds(row, 8)
        u, w, v = up[here, :], wp[here, :], vp[here, :]
        dn = v - lower(vp, row, v)
        rt_ = v - pltpu.roll(v, EW - 1, 1)
        edge = ((s == 0) & (r == 0) & (rows8 == 0)).astype(F32) + ((cols8 == 0) & (z == 0)).astype(F32)
        vv = v * v
        terms = (u * u, u * v, vv, w * vv + SMOOTH * (dn * dn + rt_ * rt_ + edge * vv))
        vc[pl.ds(pl.multiple_of(s * 8, 8), 8), :] = v[:, LANE : LANE + W]
        return tuple(a + t[:, LANE : LANE + W] for a, t in zip(acc, terms))

    acc = lax.fori_loop(0, H // 8, add_up, tuple(jnp.zeros((8, W), F32) for _ in range(4)))
    lane = iota((1, LANE), 1)
    packed = jnp.zeros((1, LANE), F32)
    for k, a in enumerate(acc):
        packed = jnp.where(lane == k, total(a), packed)
    msg[0] = packed

    def exchange(mine, slots, me, number, device, send_sem, recv_sem):
        copies = [
            pltpu.make_async_remote_copy(
                src_ref=mine, dst_ref=slots.at[me], send_sem=send_sem, recv_sem=recv_sem,
                device_id=device(lax.rem(me + k, number)), device_id_type=MESH,
            )
            for k in range(1, number)
        ]
        for c in copies:
            c.start()
        slots[me] = mine[...]

    def settle(slots, number, sems):
        arrivals = slots.at[pl.ds(0, number - 1)]
        for sem in sems:
            pltpu.make_async_copy(arrivals, arrivals, sem).wait()

    exchange(msg.at[0], slots_p, r, ROWS, lambda i: (i, z), p_send, p_recv)

    wide = []

    def wide_copy(src_rows, src_cols, dst_rows, dst_cols, device, send_if, recv_if):
        for buf in (fb, wb):
            k = len(wide)
            c = pltpu.make_async_remote_copy(
                src_ref=buf.at[src_rows, src_cols], dst_ref=buf.at[dst_rows, dst_cols],
                send_sem=wide_send.at[k], recv_sem=wide_recv.at[k], device_id=device, device_id_type=MESH,
            )
            wide.append((c, send_if, recv_if))

    first, last, every = pl.ds(HB, HB), pl.ds(H, HB), pl.ds(HB, H)
    top, below = pl.ds(0, HB), pl.ds(HB + H, HB)
    wide_copy(every, c_first, every, rt, (r, z_lf), has_lf, has_rt)
    wide_copy(every, c_last, every, lf, (r, z_rt), has_rt, has_lf)
    wide_copy(first, mid, below, mid, (r_up, z), has_up, has_dn)
    wide_copy(last, mid, top, mid, (r_dn, z), has_dn, has_up)
    wide_copy(first, c_first, below, rt, (r_up, z_lf), has_up & has_lf, has_dn & has_rt)
    wide_copy(first, c_last, below, lf, (r_up, z_rt), has_up & has_rt, has_dn & has_lf)
    wide_copy(last, c_first, top, rt, (r_dn, z_lf), has_dn & has_lf, has_up & has_rt)
    wide_copy(last, c_last, top, lf, (r_dn, z_rt), has_dn & has_rt, has_up & has_lf)
    for c, send_if, _ in wide:
        pl.when(send_if)(c.start)

    settle(slots_p, ROWS, (p_send, p_recv))
    msg[1] = jnp.sum(slots_p[...], axis=0)
    exchange(msg.at[1], slots_z, z, COLS, lambda i: (r, i), z_send, z_recv)

    def square(height, width):
        return iota((height, width), 0), iota((height, width), 1)

    i, k = square(H, 256)
    at = r * H - REACH + k
    one = jnp.where((at >= 0) & (at < ROWS * H), tap(k - REACH - i), 0.0)
    k, j = square(256, 256)
    high, low = split(dot32(one, tap(k - j)))
    row_taps[0:H, :] = high
    row_taps[H : 2 * H, :] = low
    for n, t in enumerate((0, 3, 7)):
        j, k = square(256, 256)
        at = z * W + t * LANE - REACH + k
        one = jnp.where((at >= 0) & (at < COLS * W), tap(j - k), 0.0)
        k, i = square(256, LANE)
        high, low = split(dot32(one, tap(k - REACH - i)))
        col_taps[n, :, 0:LANE] = high
        col_taps[n, :, LANE : 2 * LANE] = low

    for c, _, recv_if in wide:
        pl.when(recv_if)(c.wait_recv)

    def inside(row):
        at_row, at_col = rows8 + row + (r * H - HB), cols8 + z * W
        return (at_row >= 0) & (at_row < ROWS * H) & (at_col >= 0) & (at_col < COLS * W)

    def weighted(s, _):
        row = pl.multiple_of(s * 8, 8)
        here = pl.ds(row, 8)
        ub[here, :] = jnp.where(inside(row), fb[here, :] * wb[here, :], 0.0)
        return 0

    lax.fori_loop(0, BH // 8, weighted, 0)

    def extend(s, _):
        row = pl.multiple_of(s * 8 + 8, 8)
        here, there = pl.ds(row, 8), pl.ds(pl.multiple_of(s * 8, 8), 8)
        keep = inside(row)
        u = ub[here, :]
        v = jnp.where(keep, operator(ub, row, u, wb[here, :]), 0.0)
        f = jnp.where(keep, fb[here, :], 0.0)
        for dst, x in ((fx, f), (ux, u), (vx, v)):
            dst[there, :] = pltpu.roll(x, EW - (LANE - REACH), 1)[:, 0:SW]
        return 0

    lax.fori_loop(0, SH // 8, extend, 0)

    settle(slots_z, COLS, (z_send, z_recv))
    sums[...] = jnp.sum(slots_z[...], axis=0)

    for c, send_if, _ in near + wide:
        pl.when(send_if)(c.wait_send)


def blur_kernel(fx, ux, vx, uc, vc, row_taps, col_taps, sums, background, rms):
    g = sums[...]
    uu, uau, vv, vav = (g[0:1, k : k + 1] for k in range(4))
    alpha = uu / uau
    new = alpha * alpha * vv - uu
    keep = 1.0 + new / uu
    curve = keep * keep * uau - 2.0 * keep * alpha * vv + alpha * alpha * vav
    alpha1 = new / curve
    on_u = alpha + alpha1 * keep
    on_v = alpha1 * alpha
    background[...] = on_u * uc[...] - on_v * vc[...]
    taps_hl, taps_h = row_taps[...], row_taps[0:H, :]
    wide = SW // 2
    parts = []
    for start in (0, wide // LANE * LANE, SW):
        parts.append(start)
    highs, lows = [], []
    for a, b in zip(parts[:-1], parts[1:]):
        s = fx[:, a:b] - (on_u * ux[:, a:b] - on_v * vx[:, a:b])
        high, low = split(s * s)
        both = jnp.dot(taps_hl, high, preferred_element_type=F32)
        y = both[0:H] + both[H : 2 * H] + jnp.dot(taps_h, low, preferred_element_type=F32)
        high, low = split(y)
        highs.append(high)
        lows.append(low)
    yh, yl = jnp.concatenate(highs, axis=1), jnp.concatenate(lows, axis=1)
    for t in range(W // LANE):
        n = 0 if t == 0 else 2 if t == W // LANE - 1 else 1
        window = slice(t * LANE, t * LANE + 256)
        both = jnp.dot(yh[:, window], col_taps[n], preferred_element_type=F32)
        out = both[:, 0:LANE] + both[:, LANE:]
        out = out + jnp.dot(yl[:, window], col_taps[n, :, 0:LANE], preferred_element_type=F32)
        rms[:, t * LANE : (t + 1) * LANE] = jnp.sqrt(out + 1e-06)


def block(coadd_flux, inverse_variance, source_mask):
    vmem = pl.BlockSpec(memory_space=pltpu.VMEM)
    anywhere = pl.BlockSpec(memory_space=pl.ANY)
    fields = [jax.ShapeDtypeStruct((SH, SW), F32)] * 3 + [jax.ShapeDtypeStruct((H, W), F32)] * 2
    fields += [jax.ShapeDtypeStruct((2 * H, 256), BF16), jax.ShapeDtypeStruct((3, 256, 256), BF16)]
    fields += [jax.ShapeDtypeStruct((1, LANE), F32)]
    dma = pltpu.SemaphoreType.DMA
    mids = pl.pallas_call(
        gather_kernel,
        out_shape=fields,
        in_specs=[anywhere] * 3,
        out_specs=[vmem] * len(fields),
        scratch_shapes=[
            pltpu.VMEM((BH, EW), F32), pltpu.VMEM((BH, EW), F32), pltpu.VMEM((BH, EW), F32),
            pltpu.VMEM((H, W), F32), pltpu.VMEM((H, W), jnp.int32),
            pltpu.VMEM((PH, EW), F32), pltpu.VMEM((PH, EW), F32), pltpu.VMEM((PH, EW), F32),
            pltpu.VMEM((3, 8, LANE), F32), pltpu.VMEM((3, 8, LANE), F32),
            pltpu.VMEM((2, 1, LANE), F32), pltpu.VMEM((ROWS, 1, LANE), F32), pltpu.VMEM((COLS, 1, LANE), F32),
            dma((3,)), dma((9,)), dma((9,)), dma((16,)), dma((16,)), dma, dma, dma, dma,
        ],
        compiler_params=pltpu.CompilerParams(collective_id=0, has_side_effects=True),
        name="gather",
    )(coadd_flux, inverse_variance, source_mask)
    return pl.pallas_call(
        blur_kernel,
        out_shape=[jax.ShapeDtypeStruct((H, W), F32)] * 2,
        in_specs=[vmem] * len(fields),
        out_specs=[vmem] * 2,
        name="blur",
    )(*mids)


def solution(mesh):
    return jax.shard_map(
        block,
        mesh=mesh,
        in_specs=(P("rows", "cols"),) * 3,
        out_specs=(P("rows", "cols"),) * 2,
        check_vma=False,
    )
```

time: 407 us -> 46.5 us (0.11); the launches traced: 402 us -> 46.1 us
  blocking collectives: 314 us -> 0 us
  starting transfers between devices: 48 us -> 0 us
  Pallas kernels: 0 us -> 45.5 us
  waiting for transfers between devices: 16.9 us -> 0 us
  matrix products: 10.9 us -> 0 us
  other arithmetic: 6.39 us -> 0 us
  between operations: 4.97 us -> 0.64 us
    psum x3 -> x0, blocking collectives: 314 us -> none  [the longest x2 211 us: squares(): return lax.psum(jnp.sum(residual * residual), ('rows', 'cols'))]
    ppermute x16 -> x0, starting transfers between devices: 48 us -> none  [the longest x8 31.6 us: padded_2(): lax.ppermute(lax.slice_in_dim(block, block.shape[dim] - width, None, axis...]
    pallas_call x0 -> x2, Pallas kernels: none -> 45.5 us  [the longest x1 41.2 us: block(): pl.pallas_call(gather_kernel, out_shape=fields, in_specs=[anywhere] * 3,...]
    ppermute x16 -> x0, waiting for transfers between devices: 16.9 us -> none  [the longest x8 11.8 us: padded_2(): lax.ppermute(lax.slice_in_dim(block, 0, width, axis=dim), axis, backward)]
    dot_general x4 -> x0, matrix products: 10.9 us -> none  [the longest x2 8.23 us: cols_apply(): jnp.dot(extended, tap_table(out_length).T, precision=lax.Precision.HIGHEST)]
  transfers between devices with their start and end apart: 16 -> 0, of which waited for: 8 -> 0; matrix products, arithmetic and copies ran while one was open for 0% -> 0% of each run, Pallas kernels for 0% -> 0%
where the time goes in v1:
time: 46.5 us; the launch traced here: 46.1 us
  Pallas kernels  45.5 us (98%)
  between operations  0.64 us (1%)
    pallas_call x1, Pallas kernels, block(): pl.pallas_call(gather_kernel, out_shape=fields, in_specs=[anywhere] * 3,...  41.2 us
    pallas_call x1, Pallas kernels, block(): pl.pallas_call(blur_kernel, out_shape=[jax.ShapeDtypeStruct((H, W), F32)]...  4.35 us

profile of v1, /device:TPU:1, one launch (start us, length us, event | category | flops | bytes accessed | tf_op | source)
XLA Modules:
  0.0 46.1 jit_solution(10535614682114676180)
XLA Ops:
  0.6 41.2 %gather.1 = (f32[256,1152]{1,0:T(8,128)}, f32[256,1152]{1,0:T(8,128)}, f32[256,1152]{1,0:T(8,128)}, f32[128,1024]{1,0:T(8,128)}, f32[128,1024]{1,0:T(8,128)}, /*...) custom-call(f32[128,1024]{1,0:T(8,128)} %f_hbm.1, f32[128,1024]{1,0:T(8,128)} %iv_hbm.1, ...), custom_call_target="tpu_custom_call" | custom-call | tf_op jit(solution)/shard_map/gather/pallas_call | solution.py:334
  41.8 4.3 %blur.1 = (f32[128,1024]{1,0:T(8,128)}, f32[128,1024]{1,0:T(8,128)}) custom-call(f32[256,1152]{1,0:T(8,128)} %get-tuple-element.10.fx, f32[256,1152]{1,0:T(8,128)} %get-tuple-element.11.ux, f32[256,1152]{1,0:T(8,128)} %get-tuple-element.12.vx, f32[128,1024]{1,0:T(8,128)} %get-tuple-element.13.uc, f32[128,1024]{1,0:T(8,128)} %get-tuple-element.14.vc, ...), custom_call_target="tpu_custom_call" | custom-call | tf_op jit(solution)/shard_map/blur/pallas_call | solution.py:350

commit v2 on v1

--- a/solution.py
+++ b/solution.py
@@ -53,7 +53,7 @@
     f_hbm, iv_hbm, mk_hbm,
     fx, ux, vx, uc, vc, row_taps, col_taps, sums,
     fb, wb, ub, ivb, mkb, up, wp, vp, col_out, col_in, msg, slots_p, slots_z,
-    load_sem, near_send, near_recv, wide_send, wide_recv, p_send, p_recv, z_send, z_recv,
+    load_sem, near_send, near_recv, wide_send, wide_recv, p_send, p_recv, z_send, z_recv, chain,
 ):
     r, z = lax.axis_index("rows"), lax.axis_index("cols")
     r_up, r_dn = lax.rem(r + ROWS - 1, ROWS), lax.rem(r + 1, ROWS)
@@ -76,8 +76,8 @@
     for k in range(1, ROWS):
         pl.semaphore_signal(barrier, inc=1, device_id=(lax.rem(r + k, ROWS), z), device_id_type=MESH)
         count += 1
-    for k in range(1, COLS):
-        pl.semaphore_signal(barrier, inc=1, device_id=(r, lax.rem(z + k, COLS)), device_id_type=MESH)
+    for b in (z_lf, z_rt):
+        pl.semaphore_signal(barrier, inc=1, device_id=(r, b), device_id_type=MESH)
         count += 1
     for a in (r_up, r_dn):
         for b in (z_lf, z_rt):
@@ -105,6 +105,12 @@
     col_out[2] = jnp.transpose(up[8 : H + 8, W : W + LANE])[LANE - 8 : LANE, :]
 
     pl.semaphore_wait(barrier, count)
+
+    def entered(step):
+        for away in (1 << step, COLS - (1 << step)):
+            pl.semaphore_signal(chain.at[step], inc=1, device_id=(r, lax.rem(z + away, COLS)), device_id_type=MESH)
+
+    entered(0)
 
     near = []
 
@@ -131,6 +137,34 @@
     near_copy(up.at[first, c_last], up.at[below, lf], (r_up, z_rt), has_up & has_rt, has_dn & has_lf)
     for c, send_if, _ in near:
         pl.when(send_if)(c.start)
+    wide = []
+
+    def wide_copy(src_rows, src_cols, dst_rows, dst_cols, device, send_if, recv_if):
+        for buf in (fb, wb):
+            k = len(wide)
+            c = pltpu.make_async_remote_copy(
+                src_ref=buf.at[src_rows, src_cols], dst_ref=buf.at[dst_rows, dst_cols],
+                send_sem=wide_send.at[k], recv_sem=wide_recv.at[k], device_id=device, device_id_type=MESH,
+            )
+            wide.append((c, send_if, recv_if))
+
+    w_first, w_last, every = pl.ds(HB, HB), pl.ds(H, HB), pl.ds(HB, H)
+    w_top, w_below = pl.ds(0, HB), pl.ds(HB + H, HB)
+    wide_copy(every, c_first, every, rt, (r, z_lf), has_lf, has_rt)
+    wide_copy(every, c_last, every, lf, (r, z_rt), has_rt, has_lf)
+    wide_copy(w_first, mid, w_below, mid, (r_up, z), has_up, has_dn)
+    wide_copy(w_last, mid, w_top, mid, (r_dn, z), has_dn, has_up)
+    wide_copy(w_first, c_first, w_below, rt, (r_up, z_lf), has_up & has_lf, has_dn & has_rt)
+    wide_copy(w_first, c_last, w_below, lf, (r_up, z_rt), has_up & has_rt, has_dn & has_lf)
+    wide_copy(w_last, c_first, w_top, rt, (r_dn, z_lf), has_dn & has_lf, has_up & has_rt)
+    wide_copy(w_last, c_last, w_top, lf, (r_dn, z_rt), has_dn & has_rt, has_up & has_lf)
+    early = [n for n in range(len(wide)) if n not in (5, 7)]
+    late = [5, 7]
+    for n in early:
+        pl.when(wide[n][1])(wide[n][0].start)
+
+    pl.semaphore_wait(chain.at[0], 2)
+    entered(1)
     for c, _, recv_if in near:
         pl.when(recv_if)(c.wait_recv)
 
@@ -207,34 +241,10 @@
 
     exchange(msg.at[0], slots_p, r, ROWS, lambda i: (i, z), p_send, p_recv)
 
-    wide = []
-
-    def wide_copy(src_rows, src_cols, dst_rows, dst_cols, device, send_if, recv_if):
-        for buf in (fb, wb):
-            k = len(wide)
-            c = pltpu.make_async_remote_copy(
-                src_ref=buf.at[src_rows, src_cols], dst_ref=buf.at[dst_rows, dst_cols],
-                send_sem=wide_send.at[k], recv_sem=wide_recv.at[k], device_id=device, device_id_type=MESH,
-            )
-            wide.append((c, send_if, recv_if))
-
-    first, last, every = pl.ds(HB, HB), pl.ds(H, HB), pl.ds(HB, H)
-    top, below = pl.ds(0, HB), pl.ds(HB + H, HB)
-    wide_copy(every, c_first, every, rt, (r, z_lf), has_lf, has_rt)
-    wide_copy(every, c_last, every, lf, (r, z_rt), has_rt, has_lf)
-    wide_copy(first, mid, below, mid, (r_up, z), has_up, has_dn)
-    wide_copy(last, mid, top, mid, (r_dn, z), has_dn, has_up)
-    wide_copy(first, c_first, below, rt, (r_up, z_lf), has_up & has_lf, has_dn & has_rt)
-    wide_copy(first, c_last, below, lf, (r_up, z_rt), has_up & has_rt, has_dn & has_lf)
-    wide_copy(last, c_first, top, rt, (r_dn, z_lf), has_dn & has_lf, has_up & has_rt)
-    wide_copy(last, c_last, top, lf, (r_dn, z_rt), has_dn & has_rt, has_up & has_lf)
-    for c, send_if, _ in wide:
-        pl.when(send_if)(c.start)
-
-    settle(slots_p, ROWS, (p_send, p_recv))
-    msg[1] = jnp.sum(slots_p[...], axis=0)
-    exchange(msg.at[1], slots_z, z, COLS, lambda i: (r, i), z_send, z_recv)
-
+    for n in late:
+        pl.when(wide[n][1])(wide[n][0].start)
+    pl.semaphore_wait(chain.at[1], 2)
+    entered(2)
     def square(height, width):
         return iota((height, width), 0), iota((height, width), 1)
 
@@ -253,6 +263,11 @@
         high, low = split(dot32(one, tap(k - REACH - i)))
         col_taps[n, :, 0:LANE] = high
         col_taps[n, :, LANE : 2 * LANE] = low
+
+    settle(slots_p, ROWS, (p_send, p_recv))
+    msg[1] = jnp.sum(slots_p[...], axis=0)
+    pl.semaphore_wait(chain.at[2], 2)
+    exchange(msg.at[1], slots_z, z, COLS, lambda i: (r, i), z_send, z_recv)
 
     for c, _, recv_if in wide:
         pl.when(recv_if)(c.wait_recv)
@@ -326,7 +341,7 @@
 
 def block(coadd_flux, inverse_variance, source_mask):
     vmem = pl.BlockSpec(memory_space=pltpu.VMEM)
-    anywhere = pl.BlockSpec(memory_space=pl.ANY)
+    anywhere = pl.BlockSpec(memory_space=pltpu.HBM)
     fields = [jax.ShapeDtypeStruct((SH, SW), F32)] * 3 + [jax.ShapeDtypeStruct((H, W), F32)] * 2
     fields += [jax.ShapeDtypeStruct((2 * H, 256), BF16), jax.ShapeDtypeStruct((3, 256, 256), BF16)]
     fields += [jax.ShapeDtypeStruct((1, LANE), F32)]
@@ -342,16 +357,17 @@
             pltpu.VMEM((PH, EW), F32), pltpu.VMEM((PH, EW), F32), pltpu.VMEM((PH, EW), F32),
             pltpu.VMEM((3, 8, LANE), F32), pltpu.VMEM((3, 8, LANE), F32),
             pltpu.VMEM((2, 1, LANE), F32), pltpu.VMEM((ROWS, 1, LANE), F32), pltpu.VMEM((COLS, 1, LANE), F32),
-            dma((3,)), dma((9,)), dma((9,)), dma((16,)), dma((16,)), dma, dma, dma, dma,
+            dma((3,)), dma((9,)), dma((9,)), dma((16,)), dma((16,)), dma, dma, dma, dma, pltpu.SemaphoreType.REGULAR((3,)),
         ],
-        compiler_params=pltpu.CompilerParams(collective_id=0, has_side_effects=True),
+        compiler_params=pltpu.CompilerParams(collective_id=0, has_side_effects=True, vmem_limit_bytes=20 * 2**20),
         name="gather",
-    )(coadd_flux, inverse_variance, source_mask)
+    )(*(pltpu.with_memory_space_constraint(x, pltpu.HBM) for x in (coadd_flux, inverse_variance, source_mask)))
     return pl.pallas_call(
         blur_kernel,
         out_shape=[jax.ShapeDtypeStruct((H, W), F32)] * 2,
         in_specs=[vmem] * len(fields),
         out_specs=[vmem] * 2,
+        compiler_params=pltpu.CompilerParams(vmem_limit_bytes=20 * 2**20),
         name="blur",
     )(*mids)
 

time: 46.5 us -> 36.6 us (0.79)
  Pallas kernels: 45.5 us -> 35.9 us
    pallas_call x1, Pallas kernels: 41.2 us -> 33.9 us  [block(): pl.pallas_call(gather_kernel, out_shape=fields, in_specs=[anywhere] * 3,...]
    pallas_call x1, Pallas kernels: 4.35 us -> 1.94 us  [block(): pl.pallas_call(blur_kernel, out_shape=[jax.ShapeDtypeStruct((H, W), F32)]...]
where the time goes in v2:
time: 36.6 us; the launch traced here: 36.5 us
  Pallas kernels  35.9 us (98%)
  between operations  0.64 us (2%)
    pallas_call x1, Pallas kernels, block(): pl.pallas_call(gather_kernel, out_shape=fields, in_specs=[anywhere] * 3,...  33.9 us
    pallas_call x1, Pallas kernels, block(): pl.pallas_call(blur_kernel, out_shape=[jax.ShapeDtypeStruct((H, W), F32)]...  1.94 us

profile of v2, /device:TPU:1, one launch (start us, length us, event | category | flops | bytes accessed | tf_op | source)
XLA Modules:
  0.0 36.5 jit_solution(4566112729828252794)
XLA Ops:
  0.6 33.9 %gather.1 = (f32[256,1152]{1,0:T(8,128)S(1)}, f32[256,1152]{1,0:T(8,128)S(1)}, f32[256,1152]{1,0:T(8,128)S(1)}, f32[128,1024]{1,0:T(8,128)S(1)}, f32[128,1024]{1...) custom-call(f32[128,1024]{1,0:T(8,128)} %f_hbm.1, ...), custom_call_target="tpu_custom_call" | custom-call | tf_op jit(solution)/shard_map/gather/pallas_call | solution.py:349
  34.6 1.9 %blur.1 = (f32[128,1024]{1,0:T(8,128)}, f32[128,1024]{1,0:T(8,128)}) custom-call(f32[256,1152]{1,0:T(8,128)S(1)} %get-tuple-element.10.fx, f32[256,1152]{1,0:T(8,128)S(1)} %get-tuple-element.11.ux, f32[256,1152]{1,0:T(8,128)S(1)} %get-tuple-element.12.vx, f32[128,1024]{1,0:T(8,128)S(1)} %get-tuple-element.13.uc, f32[128,1024]{1,0:T(8,128)S(1)} %get-tuple-element.14.vc, ...), custom_call_target="tpu_custom_call" | custom-call | tf_op jit(solution)/shard_map/blur/pallas_call | solution.py:365

commit v3 on v2

--- a/solution.py
+++ b/solution.py
@@ -19,7 +19,6 @@
 EW = W + 2 * LANE
 BH = H + 2 * HB
 SH, SW = H + 2 * REACH, W + 2 * REACH
-PH = H + 24
 MESH = pl.DeviceIdType.MESH
 TAP_SUM = float(np.sum(np.exp(-np.arange(-RADIUS, RADIUS + 1) ** 2 / (2.0 * SIGMA * SIGMA))))
 F32 = jnp.float32
@@ -52,7 +51,7 @@
 def gather_kernel(
     f_hbm, iv_hbm, mk_hbm,
     fx, ux, vx, uc, vc, row_taps, col_taps, sums,
-    fb, wb, ub, ivb, mkb, up, wp, vp, col_out, col_in, msg, slots_p, slots_z,
+    fb, wb, ub, ivb, mkb, row_in, corner_in, col_out, col_in, msg, slots_p, slots_z,
     load_sem, near_send, near_recv, wide_send, wide_recv, p_send, p_recv, z_send, z_recv, chain,
 ):
     r, z = lax.axis_index("rows"), lax.axis_index("cols")
@@ -67,10 +66,6 @@
     ]
     for c in loads:
         c.start()
-    up[0:8, :] = jnp.zeros((8, EW), F32)
-    up[H + 8 : PH, :] = jnp.zeros((16, EW), F32)
-    wp[H + 8 : PH, :] = jnp.zeros((16, EW), F32)
-
     barrier = pltpu.get_barrier_semaphore()
     count = 0
     for k in range(1, ROWS):
@@ -89,20 +84,16 @@
 
     def weigh(s, _):
         rows = pl.ds(pl.multiple_of(s * 8, 8), 8)
+        there = pl.ds(pl.multiple_of(s * 8 + HB, 8), 8)
         w = ivb[rows, :] * (1.0 - mkb[rows, :].astype(F32))
-        wb[pl.ds(pl.multiple_of(s * 8 + HB, 8), 8), LANE : LANE + W] = w
-        here = pl.ds(pl.multiple_of(s * 8 + 8, 8), 8)
-        wp[here, LANE : LANE + W] = w
-        u = w * fb[pl.ds(pl.multiple_of(s * 8 + HB, 8), 8), LANE : LANE + W]
-        up[here, LANE : LANE + W] = u
-        uc[rows, :] = u
+        wb[there, LANE : LANE + W] = w
+        uc[rows, :] = w * fb[there, LANE : LANE + W]
         return 0
 
     lax.fori_loop(0, H // 8, weigh, 0)
-    left_cols = jnp.transpose(up[8 : H + 8, LANE : 2 * LANE])
-    col_out[0] = left_cols[0:8, :]
-    col_out[1] = jnp.transpose(wp[8 : H + 8, LANE : 2 * LANE])[0:8, :]
-    col_out[2] = jnp.transpose(up[8 : H + 8, W : W + LANE])[LANE - 8 : LANE, :]
+    col_out[0] = jnp.transpose(uc[:, 0:LANE])[0:8, :]
+    col_out[1] = jnp.transpose(wb[HB : HB + H, LANE : 2 * LANE])[0:8, :]
+    col_out[2] = jnp.transpose(uc[:, W - LANE : W])[LANE - 8 : LANE, :]
 
     pl.semaphore_wait(barrier, count)
 
@@ -122,19 +113,19 @@
         )
         near.append((c, send_if, recv_if))
 
-    first, last = pl.ds(8, 8), pl.ds(H, 8)
-    top, below = pl.ds(0, 8), pl.ds(H + 8, 8)
+    first, last = pl.ds(0, 8), pl.ds(H - 8, 8)
     mid, lf, rt = pl.ds(LANE, W), pl.ds(0, LANE), pl.ds(LANE + W, LANE)
     c_first, c_last = pl.ds(LANE, LANE), pl.ds(W, LANE)
-    near_copy(up.at[first, mid], up.at[below, mid], (r_up, z), has_up, has_dn)
-    near_copy(wp.at[first, mid], wp.at[below, mid], (r_up, z), has_up, has_dn)
-    near_copy(up.at[last, mid], up.at[top, mid], (r_dn, z), has_dn, has_up)
+    near_copy(uc.at[first], row_in.at[0], (r_up, z), has_up, has_dn)
+    near_copy(wb.at[pl.ds(HB, 8), mid], row_in.at[1], (r_up, z), has_up, has_dn)
+    near_copy(uc.at[last], row_in.at[2], (r_dn, z), has_dn, has_up)
     near_copy(col_out.at[0], col_in.at[0], (r, z_lf), has_lf, has_rt)
     near_copy(col_out.at[1], col_in.at[1], (r, z_lf), has_lf, has_rt)
     near_copy(col_out.at[2], col_in.at[2], (r, z_rt), has_rt, has_lf)
-    near_copy(up.at[last, c_first], up.at[top, rt], (r_dn, z_lf), has_dn & has_lf, has_up & has_rt)
-    near_copy(up.at[first, c_first], up.at[below, rt], (r_up, z_lf), has_up & has_lf, has_dn & has_rt)
-    near_copy(up.at[first, c_last], up.at[below, lf], (r_up, z_rt), has_up & has_rt, has_dn & has_lf)
+    block_lf, block_rt = pl.ds(0, LANE), pl.ds(W - LANE, LANE)
+    near_copy(uc.at[last, block_lf], corner_in.at[0], (r_dn, z_lf), has_dn & has_lf, has_up & has_rt)
+    near_copy(uc.at[first, block_lf], corner_in.at[1], (r_up, z_lf), has_up & has_lf, has_dn & has_rt)
+    near_copy(uc.at[first, block_rt], corner_in.at[2], (r_up, z_rt), has_up & has_rt, has_dn & has_lf)
     for c, send_if, _ in near:
         pl.when(send_if)(c.start)
     wide = []
@@ -163,6 +154,67 @@
     for n in early:
         pl.when(wide[n][1])(wide[n][0].start)
 
+    cols8 = iota((8, EW), 1) - LANE
+    rows8 = iota((8, EW), 0)
+
+    def higher(src, row, x):
+        before = src[pl.ds(pl.multiple_of(row - 8, 8), 8), :]
+        return pltpu.roll(jnp.where(rows8 == 7, before, x), 1, 0)
+
+    def lower(src, row, x):
+        after = src[pl.ds(pl.multiple_of(row + 8, 8), 8), :]
+        return pltpu.roll(jnp.where(rows8 == 0, after, x), 7, 0)
+
+    def operator(src, row, u, w):
+        above, under = higher(src, row, u), lower(src, row, u)
+        beside = above + under + pltpu.roll(u, 1, 1) + pltpu.roll(u, EW - 1, 1)
+        return w * u + SMOOTH * (4.0 * u - beside)
+
+    rows_w, cols_w = iota((8, W), 0), iota((8, W), 1)
+    lanes8 = iota((8, LANE), 1)
+
+    def fold(x):
+        x = jnp.sum(x.reshape(x.shape[0] // 8, 8, x.shape[1]), axis=0)
+        return sum(x[:, c : c + LANE] for c in range(0, x.shape[1], LANE))
+
+    def alone(s, acc):
+        rows = pl.ds(pl.multiple_of(s * 8, 8), 8)
+        u, w = uc[rows, :], wb[pl.ds(pl.multiple_of(s * 8 + HB, 8), 8), LANE : LANE + W]
+        before = uc[pl.ds(pl.multiple_of(jnp.maximum(s - 1, 0) * 8, 8), 8), :]
+        after = uc[pl.ds(pl.multiple_of(jnp.minimum(s + 1, H // 8 - 1) * 8, 8), 8), :]
+        before = jnp.where(s > 0, before, 0.0)
+        after = jnp.where(s < H // 8 - 1, after, 0.0)
+        beside = pltpu.roll(jnp.where(rows_w == 7, before, u), 1, 0)
+        beside = beside + pltpu.roll(jnp.where(rows_w == 0, after, u), 7, 0)
+        beside = beside + pltpu.roll(jnp.where(cols_w == W - 1, 0.0, u), 1, 1)
+        beside = beside + pltpu.roll(jnp.where(cols_w == 0, 0.0, u), W - 1, 1)
+        vc[rows, :] = w * u + SMOOTH * (4.0 * u - beside)
+        return acc + u * u
+
+    uu = lax.fori_loop(0, H // 8, alone, jnp.zeros((8, W), F32))
+    inner = W - 2 * LANE
+
+    def terms_of(u, w, v, right, under, edge=None):
+        vv = v * v
+        curve = w * vv + SMOOTH * ((v - right) * (v - right) + (v - under) * (v - under))
+        if edge is not None:
+            curve = curve + SMOOTH * jnp.where(edge, vv, 0.0)
+        return u * v, vv, curve
+
+    def middle(s, acc):
+        row = pl.multiple_of(s * 8, 8)
+        rows, there = pl.ds(row, 8), pl.ds(pl.multiple_of(s * 8 + HB, 8), 8)
+        v = vc[rows, LANE:W]
+        right = pltpu.roll(v, inner + LANE - 1, 1)[:, 0:inner]
+        v = v[:, 0:inner]
+        after = vc[pl.ds(pl.multiple_of(s * 8 + 8, 8), 8), LANE : W - LANE]
+        under = pltpu.roll(jnp.where(rows_w[:, 0:inner] == 0, after, v), 7, 0)
+        t = terms_of(uc[rows, LANE : W - LANE], wb[there, 2 * LANE : W], v, right, under)
+        return tuple(a + b for a, b in zip(acc, t))
+
+    acc = lax.fori_loop(1, H // 8 - 1, middle, tuple(jnp.zeros((8, inner), F32) for _ in range(3)))
+    sums4 = [fold(uu)] + [fold(a) for a in acc]
+
     pl.semaphore_wait(chain.at[0], 2)
     entered(1)
     for c, _, recv_if in near:
@@ -170,52 +222,57 @@
 
     pad = jnp.zeros((LANE - 8, LANE), F32)
 
-    def column(x, there):
-        return jnp.where(there, x, jnp.zeros_like(x))
-
-    up[8 : H + 8, LANE + W : EW] = jnp.transpose(jnp.concatenate([column(col_in[0], has_rt), pad], axis=0))
-    wp[8 : H + 8, LANE + W : EW] = jnp.transpose(jnp.concatenate([column(col_in[1], has_rt), pad], axis=0))
-    up[8 : H + 8, 0:LANE] = jnp.transpose(jnp.concatenate([pad, column(col_in[2], has_lf)], axis=0))
-
-    cols8 = iota((8, EW), 1) - LANE
-    rows8 = iota((8, EW), 0)
-
-    def higher(src, row, x):
-        before = src[pl.ds(pl.multiple_of(row - 8, 8), 8), :]
-        return pltpu.roll(jnp.where(rows8 == 7, before, x), 1, 0)
-
-    def lower(src, row, x):
-        after = src[pl.ds(pl.multiple_of(row + 8, 8), 8), :]
-        return pltpu.roll(jnp.where(rows8 == 0, after, x), 7, 0)
-
-    def operator(src, row, u, w):
-        above, under = higher(src, row, u), lower(src, row, u)
-        beside = above + under + pltpu.roll(u, 1, 1) + pltpu.roll(u, EW - 1, 1)
-        return w * u + SMOOTH * (4.0 * u - beside)
-
-    def image(s, _):
-        row = pl.multiple_of(s * 8 + 8, 8)
-        here = pl.ds(row, 8)
-        v = operator(up, row, up[here, :], wp[here, :])
-        inside = ((rows8 + s * 8 < H) | has_dn) & ((cols8 < W) | has_rt)
-        vp[here, :] = jnp.where(inside, v, 0.0)
-        return 0
-
-    lax.fori_loop(0, H // 8 + 1, image, 0)
-
-    def add_up(s, acc):
-        row = pl.multiple_of(s * 8 + 8, 8)
-        here = pl.ds(row, 8)
-        u, w, v = up[here, :], wp[here, :], vp[here, :]
-        dn = v - lower(vp, row, v)
-        rt_ = v - pltpu.roll(v, EW - 1, 1)
-        edge = ((s == 0) & (r == 0) & (rows8 == 0)).astype(F32) + ((cols8 == 0) & (z == 0)).astype(F32)
-        vv = v * v
-        terms = (u * u, u * v, vv, w * vv + SMOOTH * (dn * dn + rt_ * rt_ + edge * vv))
-        vc[pl.ds(pl.multiple_of(s * 8, 8), 8), :] = v[:, LANE : LANE + W]
-        return tuple(a + t[:, LANE : LANE + W] for a, t in zip(acc, terms))
-
-    acc = lax.fori_loop(0, H // 8, add_up, tuple(jnp.zeros((8, W), F32) for _ in range(4)))
+    def there(x, present):
+        return jnp.where(present, x, jnp.zeros_like(x))
+
+    top = there(row_in[2], has_up)
+    below, below_w = there(row_in[0], has_dn), there(row_in[1], has_dn)
+    cols_rt = jnp.transpose(jnp.concatenate([there(col_in[0], has_rt), pad], axis=0))
+    cols_rt_w = jnp.transpose(jnp.concatenate([there(col_in[1], has_rt), pad], axis=0))
+    cols_lf = jnp.transpose(jnp.concatenate([pad, there(col_in[2], has_lf)], axis=0))
+    corner_up = there(corner_in[0], has_up & has_rt)[7:8, :]
+    corner_dn = there(corner_in[1], has_dn & has_rt)
+    corner_lf = there(corner_in[2], has_dn & has_lf)
+    tile_rows, tile_cols = iota((H, LANE), 0), iota((H, LANE), 1)
+    vc[0:8, :] -= SMOOTH * jnp.where(rows_w == 0, pltpu.roll(top, 1, 0), 0.0)
+    vc[H - 8 : H, :] -= SMOOTH * jnp.where(rows_w == 7, pltpu.roll(below, 7, 0), 0.0)
+    vc[:, 0:LANE] -= SMOOTH * jnp.where(tile_cols == 0, pltpu.roll(cols_lf, 1, 1), 0.0)
+    vc[:, W - LANE : W] -= SMOOTH * jnp.where(tile_cols == LANE - 1, pltpu.roll(cols_rt, LANE - 1, 1), 0.0)
+
+    beside = jnp.where(tile_rows == 0, corner_up, pltpu.roll(cols_rt, 1, 0))
+    beside = beside + jnp.where(tile_rows == H - 1, corner_dn[0:1, :], pltpu.roll(cols_rt, H - 1, 0))
+    beside = beside + pltpu.roll(uc[:, W - LANE : W], 1, 1) + pltpu.roll(cols_rt, LANE - 1, 1)
+    v_rt = there(cols_rt_w * cols_rt + SMOOTH * (4.0 * cols_rt - beside), has_rt)
+
+    line = jnp.concatenate([corner_lf, below, corner_dn], axis=1)
+    beside = pltpu.roll(line, 1, 1)[:, LANE : LANE + W] + pltpu.roll(line, EW - 1, 1)[:, LANE : LANE + W]
+    beside = beside + pltpu.roll(uc[H - 8 : H, :], 1, 0) + pltpu.roll(below, 7, 0)
+    v_dn = there(below_w * below + SMOOTH * (4.0 * below - beside), has_dn)
+
+    def ring(rows, cols, right, under, edge):
+        here = wb[rows.start + HB : rows.stop + HB, cols.start + LANE : cols.stop + LANE]
+        t = terms_of(uc[rows, cols], here, vc[rows, cols], right, under, edge)
+        for k in range(3):
+            sums4[k + 1] = sums4[k + 1] + fold(t[k])
+
+    def shifted(x, beyond):
+        x = jnp.concatenate([x, beyond], axis=1)
+        return pltpu.roll(x, x.shape[1] - 1, 1)[:, 0 : x.shape[1] - LANE]
+
+    every_col = slice(0, W)
+    v = vc[0:8, :]
+    edge = ((rows_w == 0) & (r == 0)).astype(F32) + ((cols_w == 0) & (z == 0)).astype(F32)
+    ring(slice(0, 8), every_col, shifted(v, v_rt[0:8]), pltpu.roll(jnp.where(rows_w == 0, vc[8:16, :], v), 7, 0), None)
+    sums4[3] = sums4[3] + SMOOTH * fold(edge * v * v)
+    v = vc[H - 8 : H, :]
+    ring(slice(H - 8, H), every_col, shifted(v, v_rt[H - 8 : H]), pltpu.roll(jnp.where(rows_w == 0, v_dn, v), 7, 0), (cols_w == 0) & (z == 0))
+    body, body_next = slice(8, H - 8), slice(9, H - 7)
+    first_cols, last_cols = slice(0, LANE), slice(W - LANE, W)
+    at_left = (iota((H - 16, LANE), 1) == 0) & (z == 0)
+    ring(body, first_cols, shifted(vc[body, first_cols], vc[body, LANE : 2 * LANE]), vc[body_next, first_cols], at_left)
+    ring(body, last_cols, shifted(vc[body, last_cols], v_rt[8 : H - 8]), vc[body_next, last_cols], None)
+    acc = sums4
+
     lane = iota((1, LANE), 1)
     packed = jnp.zeros((1, LANE), F32)
     for k, a in enumerate(acc):
@@ -354,7 +411,7 @@
         scratch_shapes=[
             pltpu.VMEM((BH, EW), F32), pltpu.VMEM((BH, EW), F32), pltpu.VMEM((BH, EW), F32),
             pltpu.VMEM((H, W), F32), pltpu.VMEM((H, W), jnp.int32),
-            pltpu.VMEM((PH, EW), F32), pltpu.VMEM((PH, EW), F32), pltpu.VMEM((PH, EW), F32),
+            pltpu.VMEM((3, 8, W), F32), pltpu.VMEM((3, 8, LANE), F32),
             pltpu.VMEM((3, 8, LANE), F32), pltpu.VMEM((3, 8, LANE), F32),
             pltpu.VMEM((2, 1, LANE), F32), pltpu.VMEM((ROWS, 1, LANE), F32), pltpu.VMEM((COLS, 1, LANE), F32),
             dma((3,)), dma((9,)), dma((9,)), dma((16,)), dma((16,)), dma, dma, dma, dma, pltpu.SemaphoreType.REGULAR((3,)),

time: 36.6 us -> 34.3 us (0.937)
  Pallas kernels: 35.9 us -> 33.5 us
    pallas_call x1, Pallas kernels: 33.9 us -> 31.6 us  [block(): pl.pallas_call(gather_kernel, out_shape=fields, in_specs=[anywhere] * 3,...]
where the time goes in v3:
time: 34.3 us; the launch traced here: 34.1 us
  Pallas kernels  33.5 us (98%)
  between operations  0.64 us (2%)
    pallas_call x1, Pallas kernels, block(): pl.pallas_call(gather_kernel, out_shape=fields, in_specs=[anywhere] * 3,...  31.6 us
    pallas_call x1, Pallas kernels, block(): pl.pallas_call(blur_kernel, out_shape=[jax.ShapeDtypeStruct((H, W), F32)]...  1.94 us

profile of v3, /device:TPU:1, one launch (start us, length us, event | category | flops | bytes accessed | tf_op | source)
XLA Modules:
  0.0 34.1 jit_solution(12676079980846661031)
XLA Ops:
  0.6 31.6 %gather.1 = (f32[256,1152]{1,0:T(8,128)S(1)}, f32[256,1152]{1,0:T(8,128)S(1)}, f32[256,1152]{1,0:T(8,128)S(1)}, f32[128,1024]{1,0:T(8,128)S(1)}, f32[128,1024]{1...) custom-call(f32[128,1024]{1,0:T(8,128)} %f_hbm.1, ...), custom_call_target="tpu_custom_call" | custom-call | tf_op jit(solution)/shard_map/gather/pallas_call | solution.py:406
  32.2 1.9 %blur.1 = (f32[128,1024]{1,0:T(8,128)}, f32[128,1024]{1,0:T(8,128)}) custom-call(f32[256,1152]{1,0:T(8,128)S(1)} %get-tuple-element.10.fx, f32[256,1152]{1,0:T(8,128)S(1)} %get-tuple-element.11.ux, f32[256,1152]{1,0:T(8,128)S(1)} %get-tuple-element.12.vx, f32[128,1024]{1,0:T(8,128)S(1)} %get-tuple-element.13.uc, f32[128,1024]{1,0:T(8,128)S(1)} %get-tuple-element.14.vc, ...), custom_call_target="tpu_custom_call" | custom-call | tf_op jit(solution)/shard_map/blur/pallas_call | solution.py:422

commit v4 on v3

--- a/solution.py
+++ b/solution.py
@@ -21,6 +21,8 @@
 SH, SW = H + 2 * REACH, W + 2 * REACH
 MESH = pl.DeviceIdType.MESH
 TAP_SUM = float(np.sum(np.exp(-np.arange(-RADIUS, RADIUS + 1) ** 2 / (2.0 * SIGMA * SIGMA))))
+PLANE_ORDER = sorted(range(1, ROWS), key=lambda k: -min(k // 8, 4 - k // 8) - min(k % 8 // 2, 4 - k % 8 // 2))
+COLUMN_ORDER = sorted(range(1, COLS), key=lambda k: -min(k, COLS - k))
 F32 = jnp.float32
 BF16 = jnp.bfloat16
 
@@ -68,16 +70,16 @@
         c.start()
     barrier = pltpu.get_barrier_semaphore()
     count = 0
-    for k in range(1, ROWS):
+    for a in (r_up, r_dn):
+        for b in (z_lf, z_rt):
+            pl.semaphore_signal(barrier, inc=1, device_id=(a, b), device_id_type=MESH)
+            count += 1
+    for k in PLANE_ORDER:
         pl.semaphore_signal(barrier, inc=1, device_id=(lax.rem(r + k, ROWS), z), device_id_type=MESH)
         count += 1
     for b in (z_lf, z_rt):
         pl.semaphore_signal(barrier, inc=1, device_id=(r, b), device_id_type=MESH)
         count += 1
-    for a in (r_up, r_dn):
-        for b in (z_lf, z_rt):
-            pl.semaphore_signal(barrier, inc=1, device_id=(a, b), device_id_type=MESH)
-            count += 1
 
     for c in loads:
         c.wait()
@@ -285,7 +287,7 @@
                 src_ref=mine, dst_ref=slots.at[me], send_sem=send_sem, recv_sem=recv_sem,
                 device_id=device(lax.rem(me + k, number)), device_id_type=MESH,
             )
-            for k in range(1, number)
+            for k in (PLANE_ORDER if number == ROWS else COLUMN_ORDER)
         ]
         for c in copies:
             c.start()
@@ -361,7 +363,7 @@
         pl.when(send_if)(c.wait_send)
 
 
-def blur_kernel(fx, ux, vx, uc, vc, row_taps, col_taps, sums, background, rms):
+def blur_kernel(fx, ux, vx, uc, vc, row_taps, col_taps, sums, background, rms, field, scatter, sem):
     g = sums[...]
     uu, uau, vv, vav = (g[0:1, k : k + 1] for k in range(4))
     alpha = uu / uau
@@ -371,7 +373,9 @@
     alpha1 = new / curve
     on_u = alpha + alpha1 * keep
     on_v = alpha1 * alpha
-    background[...] = on_u * uc[...] - on_v * vc[...]
+    field[...] = on_u * uc[...] - on_v * vc[...]
+    writes = [pltpu.make_async_copy(field, background, sem.at[0])]
+    writes[0].start()
     taps_hl, taps_h = row_taps[...], row_taps[0:H, :]
     wide = SW // 2
     parts = []
@@ -393,7 +397,13 @@
         both = jnp.dot(yh[:, window], col_taps[n], preferred_element_type=F32)
         out = both[:, 0:LANE] + both[:, LANE:]
         out = out + jnp.dot(yl[:, window], col_taps[n, :, 0:LANE], preferred_element_type=F32)
-        rms[:, t * LANE : (t + 1) * LANE] = jnp.sqrt(out + 1e-06)
+        scatter[:, t * LANE : (t + 1) * LANE] = jnp.sqrt(out + 1e-06)
+        if t % 2:
+            pair = pl.ds((t - 1) * LANE, 2 * LANE)
+            writes.append(pltpu.make_async_copy(scatter.at[:, pair], rms.at[:, pair], sem.at[1 + t // 2]))
+            writes[-1].start()
+    for c in writes:
+        c.wait()
 
 
 def block(coadd_flux, inverse_variance, source_mask):
@@ -423,7 +433,8 @@
         blur_kernel,
         out_shape=[jax.ShapeDtypeStruct((H, W), F32)] * 2,
         in_specs=[vmem] * len(fields),
-        out_specs=[vmem] * 2,
+        out_specs=[anywhere] * 2,
+        scratch_shapes=[pltpu.VMEM((H, W), F32), pltpu.VMEM((H, W), F32), pltpu.SemaphoreType.DMA((1 + W // LANE // 2,))],
         compiler_params=pltpu.CompilerParams(vmem_limit_bytes=20 * 2**20),
         name="blur",
     )(*mids)

time: 34.3 us -> 33.5 us (0.977)
  Pallas kernels: 33.5 us -> 32.7 us
    pallas_call x1, Pallas kernels: 31.6 us -> 30.9 us  [block(): pl.pallas_call(gather_kernel, out_shape=fields, in_specs=[anywhere] * 3,...]
where the time goes in v4:
time: 33.5 us; the launch traced here: 33.4 us
  Pallas kernels  32.7 us (98%)
  between operations  0.64 us (2%)
    pallas_call x1, Pallas kernels, block(): pl.pallas_call(gather_kernel, out_shape=fields, in_specs=[anywhere] * 3,...  30.9 us
    pallas_call x1, Pallas kernels, block(): pl.pallas_call(blur_kernel, out_shape=[jax.ShapeDtypeStruct((H, W), F32)]...  1.85 us

profile of v4, /device:TPU:1, one launch (start us, length us, event | category | flops | bytes accessed | tf_op | source)
XLA Modules:
  0.0 33.4 jit_solution(13507949431018169216)
XLA Ops:
  0.6 30.9 %gather.1 = (f32[256,1152]{1,0:T(8,128)S(1)}, f32[256,1152]{1,0:T(8,128)S(1)}, f32[256,1152]{1,0:T(8,128)S(1)}, f32[128,1024]{1,0:T(8,128)S(1)}, f32[128,1024]{1...) custom-call(f32[128,1024]{1,0:T(8,128)} %f_hbm.1, ...), custom_call_target="tpu_custom_call" | custom-call | tf_op jit(solution)/shard_map/gather/pallas_call | solution.py:416
  31.5 1.8 %blur.1 = (f32[128,1024]{1,0:T(8,128)}, f32[128,1024]{1,0:T(8,128)}) custom-call(f32[256,1152]{1,0:T(8,128)S(1)} %get-tuple-element.10.fx, f32[256,1152]{1,0:T(8,128)S(1)} %get-tuple-element.11.ux, f32[256,1152]{1,0:T(8,128)S(1)} %get-tuple-element.12.vx, f32[128,1024]{1,0:T(8,128)S(1)} %get-tuple-element.13.uc, f32[128,1024]{1,0:T(8,128)S(1)} %get-tuple-element.14.vc, ...), custom_call_target="tpu_custom_call" | custom-call | tf_op jit(solution)/shard_map/blur/pallas_call | solution.py:432

commit v5 on v4

--- a/solution.py
+++ b/solution.py
@@ -53,7 +53,7 @@
 def gather_kernel(
     f_hbm, iv_hbm, mk_hbm,
     fx, ux, vx, uc, vc, row_taps, col_taps, sums,
-    fb, wb, ub, ivb, mkb, row_in, corner_in, col_out, col_in, msg, slots_p, slots_z,
+    fb, wb, ub, ivb, mkb, scaled, row_in, corner_in, col_out, col_in, msg, slots_p, slots_z,
     load_sem, near_send, near_recv, wide_send, wide_recv, p_send, p_recv, z_send, z_recv, chain,
 ):
     r, z = lax.axis_index("rows"), lax.axis_index("cols")
@@ -190,32 +190,47 @@
         beside = beside + pltpu.roll(jnp.where(rows_w == 0, after, u), 7, 0)
         beside = beside + pltpu.roll(jnp.where(cols_w == W - 1, 0.0, u), 1, 1)
         beside = beside + pltpu.roll(jnp.where(cols_w == 0, 0.0, u), W - 1, 1)
-        vc[rows, :] = w * u + SMOOTH * (4.0 * u - beside)
-        return acc + u * u
-
-    uu = lax.fori_loop(0, H // 8, alone, jnp.zeros((8, W), F32))
+        v = w * u + SMOOTH * (4.0 * u - beside)
+        vc[rows, :] = v
+        return acc[0] + u * u, acc[1] + u * v, acc[2] + v * v
+
+    uu, uv, vv = lax.fori_loop(0, H // 8, alone, (jnp.zeros((8, W), F32),) * 3)
+
+    def quotient(a, b):
+        return jnp.where(b > 0.0, a / jnp.where(b > 0.0, b, 1.0), 0.0)
+
+    near_step = quotient(total(fold(uv)), total(fold(vv)))
+
+    def scale(s, _):
+        rows = pl.ds(pl.multiple_of(s * 8, 8), 8)
+        scaled[rows, :] = uc[rows, :] - near_step * vc[rows, :]
+        return 0
+
+    lax.fori_loop(0, H // 8, scale, 0)
     inner = W - 2 * LANE
 
-    def terms_of(u, w, v, right, under, edge=None):
-        vv = v * v
-        curve = w * vv + SMOOTH * ((v - right) * (v - right) + (v - under) * (v - under))
-        if edge is not None:
-            curve = curve + SMOOTH * jnp.where(edge, vv, 0.0)
-        return u * v, vv, curve
+    def curved(w, x, right, under):
+        return w * (x * x) + SMOOTH * ((x - right) * (x - right) + (x - under) * (x - under))
 
     def middle(s, acc):
         row = pl.multiple_of(s * 8, 8)
         rows, there = pl.ds(row, 8), pl.ds(pl.multiple_of(s * 8 + HB, 8), 8)
-        v = vc[rows, LANE:W]
-        right = pltpu.roll(v, inner + LANE - 1, 1)[:, 0:inner]
-        v = v[:, 0:inner]
-        after = vc[pl.ds(pl.multiple_of(s * 8 + 8, 8), 8), LANE : W - LANE]
-        under = pltpu.roll(jnp.where(rows_w[:, 0:inner] == 0, after, v), 7, 0)
-        t = terms_of(uc[rows, LANE : W - LANE], wb[there, 2 * LANE : W], v, right, under)
-        return tuple(a + b for a, b in zip(acc, t))
-
-    acc = lax.fori_loop(1, H // 8 - 1, middle, tuple(jnp.zeros((8, inner), F32) for _ in range(3)))
-    sums4 = [fold(uu)] + [fold(a) for a in acc]
+        next_rows = pl.ds(pl.multiple_of(s * 8 + 8, 8), 8)
+        u, w = uc[rows, LANE : W - LANE], wb[there, 2 * LANE : W]
+
+        def parts(ref):
+            x = ref[rows, LANE:W]
+            right = pltpu.roll(x, inner + LANE - 1, 1)[:, 0:inner]
+            x = x[:, 0:inner]
+            under = pltpu.roll(jnp.where(rows_w[:, 0:inner] == 0, ref[next_rows, LANE : W - LANE], x), 7, 0)
+            return x, x * x, curved(w, x, right, under)
+
+        v, vv, vav = parts(vc)
+        _, ss, sas = parts(scaled)
+        return tuple(a + b for a, b in zip(acc, (u * v, vv, vav, ss, sas)))
+
+    acc = lax.fori_loop(1, H // 8 - 1, middle, tuple(jnp.zeros((8, inner), F32) for _ in range(5)))
+    tallies = [fold(uu)] + [fold(a) for a in acc]
 
     pl.semaphore_wait(chain.at[0], 2)
     entered(1)
@@ -236,10 +251,14 @@
     corner_dn = there(corner_in[1], has_dn & has_rt)
     corner_lf = there(corner_in[2], has_dn & has_lf)
     tile_rows, tile_cols = iota((H, LANE), 0), iota((H, LANE), 1)
-    vc[0:8, :] -= SMOOTH * jnp.where(rows_w == 0, pltpu.roll(top, 1, 0), 0.0)
-    vc[H - 8 : H, :] -= SMOOTH * jnp.where(rows_w == 7, pltpu.roll(below, 7, 0), 0.0)
-    vc[:, 0:LANE] -= SMOOTH * jnp.where(tile_cols == 0, pltpu.roll(cols_lf, 1, 1), 0.0)
-    vc[:, W - LANE : W] -= SMOOTH * jnp.where(tile_cols == LANE - 1, pltpu.roll(cols_rt, LANE - 1, 1), 0.0)
+    for rows, cols, change in (
+        (slice(0, 8), slice(0, W), jnp.where(rows_w == 0, pltpu.roll(top, 1, 0), 0.0)),
+        (slice(H - 8, H), slice(0, W), jnp.where(rows_w == 7, pltpu.roll(below, 7, 0), 0.0)),
+        (slice(0, H), slice(0, LANE), jnp.where(tile_cols == 0, pltpu.roll(cols_lf, 1, 1), 0.0)),
+        (slice(0, H), slice(W - LANE, W), jnp.where(tile_cols == LANE - 1, pltpu.roll(cols_rt, LANE - 1, 1), 0.0)),
+    ):
+        vc[rows, cols] -= SMOOTH * change
+        scaled[rows, cols] += near_step * (SMOOTH * change)
 
     beside = jnp.where(tile_rows == 0, corner_up, pltpu.roll(cols_rt, 1, 0))
     beside = beside + jnp.where(tile_rows == H - 1, corner_dn[0:1, :], pltpu.roll(cols_rt, H - 1, 0))
@@ -251,34 +270,44 @@
     beside = beside + pltpu.roll(uc[H - 8 : H, :], 1, 0) + pltpu.roll(below, 7, 0)
     v_dn = there(below_w * below + SMOOTH * (4.0 * below - beside), has_dn)
 
-    def ring(rows, cols, right, under, edge):
-        here = wb[rows.start + HB : rows.stop + HB, cols.start + LANE : cols.stop + LANE]
-        t = terms_of(uc[rows, cols], here, vc[rows, cols], right, under, edge)
-        for k in range(3):
-            sums4[k + 1] = sums4[k + 1] + fold(t[k])
-
     def shifted(x, beyond):
         x = jnp.concatenate([x, beyond], axis=1)
         return pltpu.roll(x, x.shape[1] - 1, 1)[:, 0 : x.shape[1] - LANE]
 
-    every_col = slice(0, W)
-    v = vc[0:8, :]
-    edge = ((rows_w == 0) & (r == 0)).astype(F32) + ((cols_w == 0) & (z == 0)).astype(F32)
-    ring(slice(0, 8), every_col, shifted(v, v_rt[0:8]), pltpu.roll(jnp.where(rows_w == 0, vc[8:16, :], v), 7, 0), None)
-    sums4[3] = sums4[3] + SMOOTH * fold(edge * v * v)
-    v = vc[H - 8 : H, :]
-    ring(slice(H - 8, H), every_col, shifted(v, v_rt[H - 8 : H]), pltpu.roll(jnp.where(rows_w == 0, v_dn, v), 7, 0), (cols_w == 0) & (z == 0))
     body, body_next = slice(8, H - 8), slice(9, H - 7)
     first_cols, last_cols = slice(0, LANE), slice(W - LANE, W)
-    at_left = (iota((H - 16, LANE), 1) == 0) & (z == 0)
-    ring(body, first_cols, shifted(vc[body, first_cols], vc[body, LANE : 2 * LANE]), vc[body_next, first_cols], at_left)
-    ring(body, last_cols, shifted(vc[body, last_cols], v_rt[8 : H - 8]), vc[body_next, last_cols], None)
-    acc = sums4
+
+    def ring(ref, beyond, beneath):
+        x = ref[0:8, :]
+        yield x, shifted(x, beyond[0:8]), pltpu.roll(jnp.where(rows_w == 0, ref[8:16, :], x), 7, 0)
+        x = ref[H - 8 : H, :]
+        yield x, shifted(x, beyond[H - 8 : H]), pltpu.roll(jnp.where(rows_w == 0, beneath, x), 7, 0)
+        x = ref[body, first_cols]
+        yield x, shifted(x, ref[body, LANE : 2 * LANE]), ref[body_next, first_cols]
+        x = ref[body, last_cols]
+        yield x, shifted(x, beyond[8 : H - 8]), ref[body_next, last_cols]
+
+    at_left = ((cols_w == 0) & (z == 0)).astype(F32)
+    edges = (
+        ((rows_w == 0) & (r == 0)).astype(F32) + at_left, at_left,
+        ((iota((H - 16, LANE), 1) == 0) & (z == 0)).astype(F32), None,
+    )
+    areas = ((slice(0, 8), slice(0, W)), (slice(H - 8, H), slice(0, W)), (body, first_cols), (body, last_cols))
+    s_rt, s_dn = cols_rt - near_step * v_rt, below - near_step * v_dn
+    for (rows, cols), edge, of_v, of_s in zip(areas, edges, ring(vc, v_rt, v_dn), ring(scaled, s_rt, s_dn)):
+        w = wb[rows.start + HB : rows.stop + HB, cols.start + LANE : cols.stop + LANE]
+        w = w if edge is None else w + SMOOTH * edge
+        v, s = of_v[0], of_s[0]
+        new = (uc[rows, cols] * v, v * v, curved(w, *of_v), s * s, curved(w, *of_s))
+        for k in range(5):
+            tallies[k + 1] = tallies[k + 1] + fold(new[k])
+    acc = tallies
 
     lane = iota((1, LANE), 1)
     packed = jnp.zeros((1, LANE), F32)
     for k, a in enumerate(acc):
         packed = jnp.where(lane == k, total(a), packed)
+    packed = jnp.where((lane == 6) | (lane == 7), near_step, packed)
     msg[0] = packed
 
     def exchange(mine, slots, me, number, device, send_sem, recv_sem):
@@ -324,7 +353,19 @@
         col_taps[n, :, LANE : 2 * LANE] = low
 
     settle(slots_p, ROWS, (p_send, p_recv))
-    msg[1] = jnp.sum(slots_p[...], axis=0)
+
+    def merge(slots, number, over):
+        plain = jnp.sum(slots[...], axis=0)
+        step = quotient(plain[:, over : over + 1], plain[:, over + 1 : over + 2])
+        moved = jnp.zeros((1, LANE), F32)
+        for n in range(number):
+            x = slots[n]
+            a, b, old = pltpu.roll(x, 3, 1), pltpu.roll(x, 2, 1), pltpu.roll(x, LANE - 2, 1)
+            by = step - old
+            moved = moved + (x - 2.0 * by * (a - old * b) + by * by * b)
+        return jnp.where(lane < 4, plain, jnp.where(lane < 6, moved, step))
+
+    msg[1] = merge(slots_p, ROWS, 1)
     pl.semaphore_wait(chain.at[2], 2)
     exchange(msg.at[1], slots_z, z, COLS, lambda i: (r, i), z_send, z_recv)
 
@@ -357,7 +398,7 @@
     lax.fori_loop(0, SH // 8, extend, 0)
 
     settle(slots_z, COLS, (z_send, z_recv))
-    sums[...] = jnp.sum(slots_z[...], axis=0)
+    sums[...] = merge(slots_z, COLS, 0)
 
     for c, send_if, _ in near + wide:
         pl.when(send_if)(c.wait_send)
@@ -365,11 +406,11 @@
 
 def blur_kernel(fx, ux, vx, uc, vc, row_taps, col_taps, sums, background, rms, field, scatter, sem):
     g = sums[...]
-    uu, uau, vv, vav = (g[0:1, k : k + 1] for k in range(4))
+    uu, uau, vv, _, new, rar = (g[0:1, k : k + 1] for k in range(6))
     alpha = uu / uau
-    new = alpha * alpha * vv - uu
-    keep = 1.0 + new / uu
-    curve = keep * keep * uau - 2.0 * keep * alpha * vv + alpha * alpha * vav
+    beta = new / uu
+    keep = 1.0 + beta
+    curve = rar + 2.0 * beta * (uau - alpha * vv) + beta * beta * uau
     alpha1 = new / curve
     on_u = alpha + alpha1 * keep
     on_v = alpha1 * alpha
@@ -421,7 +462,7 @@
         scratch_shapes=[
             pltpu.VMEM((BH, EW), F32), pltpu.VMEM((BH, EW), F32), pltpu.VMEM((BH, EW), F32),
             pltpu.VMEM((H, W), F32), pltpu.VMEM((H, W), jnp.int32),
-            pltpu.VMEM((3, 8, W), F32), pltpu.VMEM((3, 8, LANE), F32),
+            pltpu.VMEM((H, W), F32), pltpu.VMEM((3, 8, W), F32), pltpu.VMEM((3, 8, LANE), F32),
             pltpu.VMEM((3, 8, LANE), F32), pltpu.VMEM((3, 8, LANE), F32),
             pltpu.VMEM((2, 1, LANE), F32), pltpu.VMEM((ROWS, 1, LANE), F32), pltpu.VMEM((COLS, 1, LANE), F32),
             dma((3,)), dma((9,)), dma((9,)), dma((16,)), dma((16,)), dma, dma, dma, dma, pltpu.SemaphoreType.REGULAR((3,)),

time: 33.5 us -> 34.4 us (1.027)
  Pallas kernels: 32.7 us -> 33.6 us
    pallas_call x1, Pallas kernels: 30.9 us -> 31.5 us  [block(): pl.pallas_call(gather_kernel, out_shape=fields, in_specs=[anywhere] * 3,...]
where the time goes in v5:
time: 34.4 us; the launch traced here: 34.3 us
  Pallas kernels  33.6 us (98%)
  between operations  0.64 us (2%)
    pallas_call x1, Pallas kernels, block(): pl.pallas_call(gather_kernel, out_shape=fields, in_specs=[anywhere] * 3,...  31.5 us
    pallas_call x1, Pallas kernels, block(): pl.pallas_call(blur_kernel, out_shape=[jax.ShapeDtypeStruct((H, W), F32)]...  2.13 us

profile of v5, /device:TPU:1, one launch (start us, length us, event | category | flops | bytes accessed | tf_op | source)
XLA Modules:
  0.0 34.3 jit_solution(16590680132513233876)
XLA Ops:
  0.6 31.5 %gather.1 = (f32[256,1152]{1,0:T(8,128)S(1)}, f32[256,1152]{1,0:T(8,128)S(1)}, f32[256,1152]{1,0:T(8,128)S(1)}, f32[128,1024]{1,0:T(8,128)S(1)}, f32[128,1024]{1...) custom-call(f32[128,1024]{1,0:T(8,128)} %f_hbm.1, ...), custom_call_target="tpu_custom_call" | custom-call | tf_op jit(solution)/shard_map/gather/pallas_call | solution.py:457
  32.1 2.1 %blur.1 = (f32[128,1024]{1,0:T(8,128)}, f32[128,1024]{1,0:T(8,128)}) custom-call(f32[256,1152]{1,0:T(8,128)S(1)} %get-tuple-element.10.fx, f32[256,1152]{1,0:T(8,128)S(1)} %get-tuple-element.11.ux, f32[256,1152]{1,0:T(8,128)S(1)} %get-tuple-element.12.vx, f32[128,1024]{1,0:T(8,128)S(1)} %get-tuple-element.13.uc, f32[128,1024]{1,0:T(8,128)S(1)} %get-tuple-element.14.vc, ...), custom_call_target="tpu_custom_call" | custom-call | tf_op jit(solution)/shard_map/blur/pallas_call | solution.py:473

commit v6 on v5

--- a/solution.py
+++ b/solution.py
@@ -209,6 +209,9 @@
     lax.fori_loop(0, H // 8, scale, 0)
     inner = W - 2 * LANE
 
+    pl.semaphore_wait(chain.at[0], 2)
+    entered(1)
+
     def curved(w, x, right, under):
         return w * (x * x) + SMOOTH * ((x - right) * (x - right) + (x - under) * (x - under))
 
@@ -232,8 +235,6 @@
     acc = lax.fori_loop(1, H // 8 - 1, middle, tuple(jnp.zeros((8, inner), F32) for _ in range(5)))
     tallies = [fold(uu)] + [fold(a) for a in acc]
 
-    pl.semaphore_wait(chain.at[0], 2)
-    entered(1)
     for c, _, recv_if in near:
         pl.when(recv_if)(c.wait_recv)
 
@@ -355,14 +356,12 @@
     settle(slots_p, ROWS, (p_send, p_recv))
 
     def merge(slots, number, over):
-        plain = jnp.sum(slots[...], axis=0)
+        x = slots[...].reshape(number, LANE)
+        plain = jnp.sum(x, axis=0, keepdims=True)
         step = quotient(plain[:, over : over + 1], plain[:, over + 1 : over + 2])
-        moved = jnp.zeros((1, LANE), F32)
-        for n in range(number):
-            x = slots[n]
-            a, b, old = pltpu.roll(x, 3, 1), pltpu.roll(x, 2, 1), pltpu.roll(x, LANE - 2, 1)
-            by = step - old
-            moved = moved + (x - 2.0 * by * (a - old * b) + by * by * b)
+        a, b, old = pltpu.roll(x, 3, 1), pltpu.roll(x, 2, 1), pltpu.roll(x, LANE - 2, 1)
+        by = step - old
+        moved = jnp.sum(x - 2.0 * by * (a - old * b) + by * by * b, axis=0, keepdims=True)
         return jnp.where(lane < 4, plain, jnp.where(lane < 6, moved, step))
 
     msg[1] = merge(slots_p, ROWS, 1)

time: 34.4 us -> 34.4 us (level)
  no operation moved by 1% of the time
where the time goes in v6:
time: 34.4 us; the launch traced here: 34.3 us
  Pallas kernels  33.6 us (98%)
  between operations  0.64 us (2%)
    pallas_call x1, Pallas kernels, block(): pl.pallas_call(gather_kernel, out_shape=fields, in_specs=[anywhere] * 3,...  31.5 us
    pallas_call x1, Pallas kernels, block(): pl.pallas_call(blur_kernel, out_shape=[jax.ShapeDtypeStruct((H, W), F32)]...  2.14 us

profile of v6, /device:TPU:1, one launch (start us, length us, event | category | flops | bytes accessed | tf_op | source)
XLA Modules:
  0.0 34.3 jit_solution(18204431375042740316)
XLA Ops:
  0.6 31.5 %gather.1 = (f32[256,1152]{1,0:T(8,128)S(1)}, f32[256,1152]{1,0:T(8,128)S(1)}, f32[256,1152]{1,0:T(8,128)S(1)}, f32[128,1024]{1,0:T(8,128)S(1)}, f32[128,1024]{1...) custom-call(f32[128,1024]{1,0:T(8,128)} %f_hbm.1, ...), custom_call_target="tpu_custom_call" | custom-call | tf_op jit(solution)/shard_map/gather/pallas_call | solution.py:456
  32.1 2.1 %blur.1 = (f32[128,1024]{1,0:T(8,128)}, f32[128,1024]{1,0:T(8,128)}) custom-call(f32[256,1152]{1,0:T(8,128)S(1)} %get-tuple-element.10.fx, f32[256,1152]{1,0:T(8,128)S(1)} %get-tuple-element.11.ux, f32[256,1152]{1,0:T(8,128)S(1)} %get-tuple-element.12.vx, f32[128,1024]{1,0:T(8,128)S(1)} %get-tuple-element.13.uc, f32[128,1024]{1,0:T(8,128)S(1)} %get-tuple-element.14.vc, ...), custom_call_target="tpu_custom_call" | custom-call | tf_op jit(solution)/shard_map/blur/pallas_call | solution.py:472
